TPU v7x, 512 devices: a whole 4x8x8 slice. The times are simulated.
512 devices in a mesh: row: 32 (over y, z_lo), col: 16 (over x, z_hi, core).
Axes of the slice: x: 4, y: 8, z: 8 (z_hi: 2, z_lo: 4; z = z_hi * 4 + z_lo), core: 2. Of those that a mesh axis runs over, the one named last changes fastest.
Arguments:
- covariance: float32 [8192, 8192], P('row', 'col')
- courants: float32 [2, 2, 64, 128], replicated, may hold values from -0.9 to 0.9
- process_noise_spread: float32 [64, 128], P('row'), may hold values from 0.1 to 1
- sensor_targets: int32 [512], replicated, may hold values from 0 to 8191, as said below
- noise_variance: float32 [512], replicated, may hold values from 0.2 to 1
Outputs:
- posterior_spread: float32 [8192, 8192], P('row', 'col')
Inputs may be any that keep to these rules, and one draw needn't show every extreme that they name: `sensor_targets`: sorted ascending, all distinct; exactly 16 of them lie in each band of 256 consecutive state indices that starts at a multiple of 256.
All inputs are finite; a program needn't handle non-finite values.
Results may differ from a plain program's by a relative error of at most 0.0003.
Values sent between devices are 32-bit elements; how exact they have to be, the bound alone decides.
No kernel may reach another device: no remote copies, remote signals or barrier semaphores. Data moves between devices by JAX's collectives and lax.ppermute only.
A program may use at most 64 MiB of HBM per device.

v0:
```python
import jax
import jax.numpy as jnp
from jax import lax
from jax.experimental import pallas as pl
from jax.experimental.pallas import tpu as pltpu
from jax.sharding import PartitionSpec as P

NC = 128
CYCLES = 2
TILE = 128
GROUP = 8


finest_accuracy = lax.Precision.HIGHEST


def from_everyone(array, axis):
    copies = jnp.broadcast_to(array, (lax.axis_size(axis), *array.shape))
    return lax.all_to_all(copies, axis, split_axis=0, concat_axis=0, tiled=True)


def from_neighbours(lower, upper, axis):
    size = lax.axis_size(axis)
    up = [(i, (i + 1) % size) for i in range(size)]
    down = [(j, i) for i, j in up]
    return lax.ppermute(upper, axis, up), lax.ppermute(lower, axis, down)


def stencil_weights(courant):
    return (
        courant * (1.0 + courant) * 0.5,
        1.0 - courant * courant,
        courant * (courant - 1.0) * 0.5,
    )


def sweep_local(field, courant, which_axis):
    weight_behind, weight_centre, weight_ahead = stencil_weights(courant)
    return (
        weight_behind * jnp.roll(field, 1, which_axis)
        + weight_centre * field
        + weight_ahead * jnp.roll(field, -1, which_axis)
    )


def sweep_padded(padded, courant, which_axis):
    keep = padded.shape[which_axis] - 2
    weight_behind, weight_centre, weight_ahead = stencil_weights(courant)
    return (
        weight_behind * lax.slice_in_dim(padded, 0, keep, axis=which_axis)
        + weight_centre * lax.slice_in_dim(padded, 1, keep + 1, axis=which_axis)
        + weight_ahead * lax.slice_in_dim(padded, 2, keep + 2, axis=which_axis)
    )


def wind_rows(courants, cycle, component, offset, length):
    surface = courants[cycle, component]
    doubled = jnp.concatenate([surface, surface], axis=0)
    return lax.dynamic_slice_in_dim(doubled, jnp.mod(offset, surface.shape[0]), length, 0)


def lane_spread(x, k):
    return jnp.broadcast_to(x[:, k : k + 1], x.shape)


def row_spread(x, k):
    return jnp.broadcast_to(x[k : k + 1, :], x.shape)


def tree_sum(terms):
    while len(terms) > 1:
        terms = [a + b for a, b in zip(terms[::2], terms[1::2])]
    return terms[0]


def inverse_tile(rows, lane, sub):
    rows = list(rows)
    for g in range(TILE // GROUP):
        panel = rows[g]
        first = GROUP * g
        inside = (lane >= first) & (lane < first + GROUP)
        cols = [lane_spread(panel, first + m) for m in range(GROUP)]
        for k in range(GROUP):
            here = sub == k
            flip = pl.reciprocal(row_spread(cols[k], k), approx=False)
            lead = cols[k]
            for m in range(GROUP):
                if m != k:
                    scaled = row_spread(cols[m], k) * flip
                    cols[m] = jnp.where(here, scaled, cols[m] - lead * scaled)
            cols[k] = jnp.where(here, flip, -lead * flip)
        panel = jnp.where(inside, jnp.where(lane - first == sub, 1.0, 0.0), panel)
        solved = tree_sum([cols[m] * row_spread(panel, m) for m in range(GROUP)])
        spread = [row_spread(solved, m) for m in range(GROUP)]
        for i in list(range(g + 1, len(rows))) + list(range(g)):
            change = tree_sum([lane_spread(rows[i], first + m) * spread[m] for m in range(GROUP)])
            rows[i] = jnp.where(inside, 0.0, rows[i]) - change
        rows[g] = solved
    return rows


def exact_dot(a, b):
    return jnp.dot(a, b, precision=finest_accuracy, preferred_element_type=jnp.float32)


def solve_kernel(innovation_ref, noise_ref, gain_ref, out_ref, work):
    size = innovation_ref.shape[0]
    lane = lax.broadcasted_iota(jnp.int32, (GROUP, TILE), 1)
    sub = lax.broadcasted_iota(jnp.int32, (GROUP, TILE), 0)
    square = innovation_ref[...]
    square = 0.5 * (square + square.T)
    diagonal = lax.broadcasted_iota(jnp.int32, (size, size), 0) == lax.broadcasted_iota(
        jnp.int32, (size, size), 1
    )
    work[:, :size] = jnp.where(diagonal, square + noise_ref[...], square)
    work[:, size:] = gain_ref[...]
    tiles = size // TILE
    for t in range(tiles):
        lo, hi = t * TILE, (t + 1) * TILE
        rows = [work[lo + GROUP * i : lo + GROUP * (i + 1), lo:hi] for i in range(TILE // GROUP)]
        inverse = jnp.concatenate(inverse_tile(rows, lane, sub), axis=0)
        solved = exact_dot(inverse, work[lo:hi, hi:])
        for i in range(tiles):
            if i != t:
                span = slice(i * TILE, (i + 1) * TILE)
                work[span, hi:] = work[span, hi:] - exact_dot(work[span, lo:hi], solved)
        work[lo:hi, hi:] = solved
    out_ref[...] = work[:, size:]


def solve_gain(innovation, noise, gain):
    return pl.pallas_call(
        solve_kernel,
        out_shape=jax.ShapeDtypeStruct(gain.shape, jnp.float32),
        in_specs=[pl.BlockSpec(memory_space=pltpu.VMEM)] * 3,
        out_specs=pl.BlockSpec(memory_space=pltpu.VMEM),
        scratch_shapes=[pltpu.VMEM((gain.shape[0], gain.shape[0] + gain.shape[1]), jnp.float32)],
        name="solve_gain",
    )(innovation, noise[None, :], gain)


def contract(a, b, dims):
    return lax.dot_general(a, b, (dims, ((), ())), precision=finest_accuracy)


def per_device(covariance, courants, process_noise_spread, sensor_targets, noise_variance):
    row_index = lax.axis_index("row")
    column_index = lax.axis_index("col")
    height, width = covariance.shape
    band_rows, band_columns = height // NC, width // NC
    row_first, column_first = row_index * band_rows, column_index * band_columns

    before, after = from_neighbours(
        covariance[: CYCLES * NC], covariance[height - CYCLES * NC :], "row"
    )
    field = jnp.concatenate([before, covariance, after], axis=0).reshape(-1, NC, width)
    for cycle in range(CYCLES):
        length = field.shape[0]
        offset = row_first - (CYCLES - cycle)
        field = sweep_local(field, wind_rows(courants, cycle, 0, offset, length)[:, :, None], 1)
        north = wind_rows(courants, cycle, 1, offset + 1, length - 2)[:, :, None]
        field = sweep_padded(field, north, 0)
    half_way = field.reshape(height, width)

    before, after = from_neighbours(
        half_way[:, : CYCLES * NC], half_way[:, width - CYCLES * NC :], "col"
    )
    field = jnp.concatenate([before, half_way, after], axis=1).reshape(height, -1, NC)
    for cycle in range(CYCLES):
        length = field.shape[1]
        offset = column_first - (CYCLES - cycle)
        field = sweep_local(field, wind_rows(courants, cycle, 0, offset, length)[None], 2)
        north = wind_rows(courants, cycle, 1, offset + 1, length - 2)[None]
        field = sweep_padded(field, north, 1)
    forecast = field.reshape(height, width)

    row_ids = row_index * height + jnp.arange(height, dtype=jnp.int32)
    column_ids = column_index * width + jnp.arange(width, dtype=jnp.int32)
    forecast = forecast + jnp.where(
        row_ids[:, None] == column_ids[None, :], process_noise_spread.reshape(height, 1), 0.0
    )

    sensors = sensor_targets.shape[0]
    row_share = sensors // lax.axis_size("row")
    column_share = sensors // lax.axis_size("col")
    row_sensors = lax.dynamic_slice_in_dim(sensor_targets, row_index * row_share, row_share)
    column_sensors = lax.dynamic_slice_in_dim(
        sensor_targets, column_index * column_share, column_share
    )
    pick_rows = (row_sensors[:, None] == row_ids[None, :]).astype(jnp.float32)
    pick_columns = (column_sensors[:, None] == column_ids[None, :]).astype(jnp.float32)

    gain = from_everyone(contract(pick_columns, forecast, ((1,), (1,))), "col")
    gain = gain.reshape(sensors, height)
    strip = contract(pick_rows, gain, ((1,), (1,)))
    innovation = from_everyone(strip, "row").reshape(sensors, sensors)
    obs_rows = from_everyone(contract(pick_rows, forecast, ((1,), (0,))), "row")
    obs_rows = obs_rows.reshape(sensors, width)
    solved = solve_gain(innovation, noise_variance, gain)
    return forecast - contract(solved, obs_rows, ((0,), (0,)))


def solution(mesh):
    in_specs = (P("row", "col"), P(), P("row", None), P(), P())
    out_specs = P("row", "col")
    return jax.shard_map(
        per_device, mesh=mesh, in_specs=in_specs, out_specs=out_specs, check_vma=False
    )
```

profile of v0, /device:TPU:16, one launch (start us, length us, event | category | flops | bytes accessed | tf_op | source)
XLA Modules:
  0.0 167.0 jit_solution(18237165632353789955)
XLA Ops:
  0.0 4.3 %collective-permute-start = (f32[256,512]{1,0:T(8,128)}, f32[256,512]{1,0:T(8,128)S(1)}, u32[]{:S(2)}, u32[]{:S(2)}) collective-permute-start(f32[256,512]{1,0:T(8,128)} %param.5), channel_id=1, source_target_pairs={{0,16},{16,32},{32,48},{48,64},{64,80},{80,96},{96,112},{112,128},... | collective-permute-start | bytes 1572872 | tf_op jit(solution)/shard_map/ppermute | solution.py:26
  4.3 5.4 %collective-permute-start.1 = (f32[256,512]{1,0:T(8,128)}, f32[256,512]{1,0:T(8,128)S(1)}, u32[]{:S(2)}, u32[]{:S(2)}) collective-permute-start(f32[256,512]{1,0:T(8,128)} %param.5), channel_id=1, source_target_pairs={{16,0},{32,16},{48,32},{64,48},{80,64},{96,80},{112,96},{128,112},... | collective-permute-start | bytes 1572872 | tf_op jit(solution)/shard_map/ppermute | solution.py:26
  9.8 0.8 slice_bitcast_fusion.3
  11.0 16.0 %collective-permute-done = f32[256,512]{1,0:T(8,128)S(1)} collective-permute-done((f32[256,512]{1,0:T(8,128)}, f32[256,512]{1,0:T(8,128)S(1)}, u32[]{:S(2)}, u32[]{:S(2)}) %collective-permute-start) | collective-permute-done | bytes 524320 | tf_op jit(solution)/shard_map/ppermute | solution.py:26
  27.0 4.1 %collective-permute-done.1 = f32[256,512]{1,0:T(8,128)S(1)} collective-permute-done((f32[256,512]{1,0:T(8,128)}, f32[256,512]{1,0:T(8,128)S(1)}, u32[]{:S(2)}, u32[]{:S(2)}) %collective-permute-start.1) | collective-permute-done | bytes 524320 | tf_op jit(solution)/shard_map/ppermute | solution.py:26
  31.1 1.2 pad_maximum_fusion
  32.3 0.4 fusion.70
  32.7 0.5 fusion.1
  33.8 0.7 fusion.7
  34.7 1.9 %collective-permute-start.2 = (f32[256,256]{1,0:T(8,128)S(1)}, f32[256,256]{1,0:T(8,128)S(1)}, u32[]{:S(2)}, u32[]{:S(2)}) collective-permute-start(f32[256,256]{1,0:T(8,128)S(1)} %get-tuple-element.37), channel_id=1, source_target_pairs={{0,1},{1,2},{2,3},{3,4},{4,5},{5,6},{6,7},{7,8},{8,9},{9,10},{10,1... | collective-permute-start | bytes 786440 | tf_op jit(solution)/shard_map/ppermute | solution.py:26
  36.7 11.3 %collective-permute-start.3 = (f32[256,256]{1,0:T(8,128)S(1)}, f32[256,256]{1,0:T(8,128)S(1)}, u32[]{:S(2)}, u32[]{:S(2)}) collective-permute-start(f32[256,256]{1,0:T(8,128)S(1)} %get-tuple-element.38), channel_id=1, source_target_pairs={{1,0},{2,1},{3,2},{4,3},{5,4},{6,5},{7,6},{8,7},{9,8},{10,9},{11,1... | collective-permute-start | bytes 786440 | tf_op jit(solution)/shard_map/ppermute | solution.py:26
  48.1 2.1 %collective-permute-done.2 = f32[256,256]{1,0:T(8,128)S(1)} collective-permute-done((f32[256,256]{1,0:T(8,128)S(1)}, f32[256,256]{1,0:T(8,128)S(1)}, u32[]{:S(2)}, u32[]{:S(2)}) %collective-permute-start.2) | collective-permute-done | bytes 262176 | tf_op jit(solution)/shard_map/ppermute | solution.py:26
  50.2 4.5 %collective-permute-done.3 = f32[256,256]{1,0:T(8,128)S(1)} collective-permute-done((f32[256,256]{1,0:T(8,128)S(1)}, f32[256,256]{1,0:T(8,128)S(1)}, u32[]{:S(2)}, u32[]{:S(2)}) %collective-permute-start.3) | collective-permute-done | bytes 262176 | tf_op jit(solution)/shard_map/ppermute | solution.py:26
  55.3 0.3 fusion.75
  55.6 0.6 fusion.9
  56.9 0.3 fusion.72
  57.3 0.9 fusion.11
  58.5 0.4 copy-done.2
  58.8 0.5 fusion.17
  59.3 0.8 broadcast_in_dim.25
  60.2 9.7 %all-to-all-start = ((f32[16,32,256]{2,1,0:T(8,128)}), f32[16,32,256]{2,1,0:T(8,128)S(1)}, u32[]{:S(2)}, u32[]{:S(2)}) async-start(f32[16,32,256]{2,1,0:T(8,128)} %broadcast_in_dim.25), calls=%async_computation | async-start | bytes 1048576 | tf_op jit(solution)/shard_map/all_to_all | solution.py:19
  69.9 14.8 %all-to-all-done = f32[16,32,256]{2,1,0:T(8,128)S(1)} async-done(((f32[16,32,256]{2,1,0:T(8,128)}), f32[16,32,256]{2,1,0:T(8,128)S(1)}, u32[]{:S(2)}, u32[]{:S(2)}) %all-to-all-start) | async-done | bytes 524320 | tf_op jit(solution)/shard_map/all_to_all | solution.py:19
  84.7 0.4 fusion.30
  85.0 1.1 broadcast_in_dim.44
  86.2 14.9 %all-to-all-start.1 = ((f32[32,16,512]{2,1,0:T(8,128)}), f32[32,16,512]{2,1,0:T(8,128)S(1)}, u32[]{:S(2)}, u32[]{:S(2)}) async-start(f32[32,16,512]{2,1,0:T(8,128)} %broadcast_in_dim.44), calls=%async_computation.1 | async-start | bytes 2097152 | tf_op jit(solution)/shard_map/all_to_all | solution.py:19
  101.1 0.4 fusion.16
  101.5 27.8 %all-to-all-done.1 = f32[32,16,512]{2,1,0:T(8,128)S(1)} async-done(((f32[32,16,512]{2,1,0:T(8,128)}), f32[32,16,512]{2,1,0:T(8,128)S(1)}, u32[]{:S(2)}, u32[]{:S(2)}) %all-to-all-start.1) | async-done | bytes 1048608 | tf_op jit(solution)/shard_map/all_to_all | solution.py:19
  129.2 1.2 broadcast_in_dim.46
  130.6 4.8 %all-to-all-start.2 = ((f32[32,16,512]{2,1,0:T(8,128)}), f32[32,16,512]{2,1,0:T(8,128)S(1)}, u32[]{:S(2)}, u32[]{:S(2)}) async-start(f32[32,16,512]{2,1,0:T(8,128)} %broadcast_in_dim.46), calls=%async_computation.2 | async-start | bytes 2097152 | tf_op jit(solution)/shard_map/all_to_all | solution.py:19
  135.4 21.9 %solve_gain.1 = f32[512,256]{1,0:T(8,128)} custom-call(f32[512,512]{1,0:T(8,128)} %bitcast.39, f32[1,512]{1,0:T(1,128)} %bitcast.43, f32[512,256]{1,0:T(8,128)} %bitcast.35), custom_call_target="tpu_custom_call" | custom-call | tf_op jit(solution)/shard_map/solve_gain/pallas_call | solution.py:132
  157.3 6.8 %all-to-all-done.2 = f32[32,16,512]{2,1,0:T(8,128)S(1)} async-done(((f32[32,16,512]{2,1,0:T(8,128)}), f32[32,16,512]{2,1,0:T(8,128)S(1)}, u32[]{:S(2)}, u32[]{:S(2)}) %all-to-all-start.2) | async-done | bytes 1048608 | tf_op jit(solution)/shard_map/all_to_all | solution.py:19
  164.1 2.9 %convolution_subtract_fusion = f32[256,512]{1,0:T(8,128)} fusion(f32[512,256]{1,0:T(8,128)} %solve_gain.1, f32[512,512]{1,0:T(8,128)S(1)} %bitcast.38, f32[32,8,4,128]{3,2,1,0:T(4,128)S(1)} %bitcast.42, f32[256]{0:T(256)S(1)} %bitcast.46, s32[512]{0:T(512)S(1)} %iota_add_fusion, s32[256]{0:T(256)S(1)} %iota_add_fusion.1), kind=kOutput, calls=%fused_computation.5 | convolution fusion | flops 805830656 | bytes 2625536 | tf_op jit(solution)/shard_map/dot_general | solution.py:143
  (38 shorter events, 2.9 us)
Async XLA Ops:
  0.0 27.0 %collective-permute-start = (f32[256,512]{1,0:T(8,128)}, f32[256,512]{1,0:T(8,128)S(1)}, u32[]{:S(2)}, u32[]{:S(2)}) collective-permute-start(f32[256,512]{1,0:T(8,128)} %param.5), channel_id=1, source_target_pairs={{0,16},{16,32},{32,48},{48,64},{64,80},{80,96},{96,112},{112,128},... | collective-permute-start | bytes 1572872 | tf_op jit(solution)/shard_map/ppermute | solution.py:26
  4.3 26.9 %collective-permute-start.1 = (f32[256,512]{1,0:T(8,128)}, f32[256,512]{1,0:T(8,128)S(1)}, u32[]{:S(2)}, u32[]{:S(2)}) collective-permute-start(f32[256,512]{1,0:T(8,128)} %param.5), channel_id=1, source_target_pairs={{16,0},{32,16},{48,32},{64,48},{80,64},{96,80},{112,96},{128,112},... | collective-permute-start | bytes 1572872 | tf_op jit(solution)/shard_map/ppermute | solution.py:26
  34.5 13.5 %copy-start.3 = (s32[512]{0:T(512)S(1)}, s32[512]{0:T(512)}, u32[]{:S(2)}) copy-start(s32[512]{0:T(512)} %param.8) | copy-start | bytes 6148
  34.7 15.4 %collective-permute-start.2 = (f32[256,256]{1,0:T(8,128)S(1)}, f32[256,256]{1,0:T(8,128)S(1)}, u32[]{:S(2)}, u32[]{:S(2)}) collective-permute-start(f32[256,256]{1,0:T(8,128)S(1)} %get-tuple-element.37), channel_id=1, source_target_pairs={{0,1},{1,2},{2,3},{3,4},{4,5},{5,6},{6,7},{7,8},{8,9},{9,10},{10,1... | collective-permute-start | bytes 786440 | tf_op jit(solution)/shard_map/ppermute | solution.py:26
  36.7 18.0 %collective-permute-start.3 = (f32[256,256]{1,0:T(8,128)S(1)}, f32[256,256]{1,0:T(8,128)S(1)}, u32[]{:S(2)}, u32[]{:S(2)}) collective-permute-start(f32[256,256]{1,0:T(8,128)S(1)} %get-tuple-element.38), channel_id=1, source_target_pairs={{1,0},{2,1},{3,2},{4,3},{5,4},{6,5},{7,6},{8,7},{9,8},{10,9},{11,1... | collective-permute-start | bytes 786440 | tf_op jit(solution)/shard_map/ppermute | solution.py:26
  58.2 0.7 copy-start.2
  60.2 24.5 %all-to-all-start = ((f32[16,32,256]{2,1,0:T(8,128)}), f32[16,32,256]{2,1,0:T(8,128)S(1)}, u32[]{:S(2)}, u32[]{:S(2)}) async-start(f32[16,32,256]{2,1,0:T(8,128)} %broadcast_in_dim.25), calls=%async_computation | async-start | bytes 1048576 | tf_op jit(solution)/shard_map/all_to_all | solution.py:19
  84.7 1.5 copy-start
  86.2 43.1 %all-to-all-start.1 = ((f32[32,16,512]{2,1,0:T(8,128)}), f32[32,16,512]{2,1,0:T(8,128)S(1)}, u32[]{:S(2)}, u32[]{:S(2)}) async-start(f32[32,16,512]{2,1,0:T(8,128)} %broadcast_in_dim.44), calls=%async_computation.1 | async-start | bytes 2097152 | tf_op jit(solution)/shard_map/all_to_all | solution.py:19
  129.2 1.4 copy-start.1
  130.6 33.5 %all-to-all-start.2 = ((f32[32,16,512]{2,1,0:T(8,128)}), f32[32,16,512]{2,1,0:T(8,128)S(1)}, u32[]{:S(2)}, u32[]{:S(2)}) async-start(f32[32,16,512]{2,1,0:T(8,128)} %broadcast_in_dim.46), calls=%async_computation.2 | async-start | bytes 2097152 | tf_op jit(solution)/shard_map/all_to_all | solution.py:19
where the time goes:
time: 168 us; the launch traced here: 167 us
  waiting for transfers between devices  76 us (45%)
  starting transfers between devices  52.3 us (31%)
  Pallas kernels  21.9 us (13%)
  local copies, waits for them, and re-layouts  6.91 us (4%)
  other arithmetic  5.28 us (3%)
  matrix products  4.15 us (2%)
    all_to_all x3, waiting for transfers between devices, from_everyone(): return lax.all_to_all(copies, axis, split_axis=0, concat_axis=0, tiled=True)  49.3 us
    all_to_all x3, starting transfers between devices, from_everyone(): return lax.all_to_all(copies, axis, split_axis=0, concat_axis=0, tiled=True)  29.4 us
    ppermute x4, waiting for transfers between devices, from_neighbours(): return (lax.ppermute(upper, axis, up), lax.ppermute(lower, axis, down))  26.7 us
    ppermute x4, starting transfers between devices, from_neighbours(): return (lax.ppermute(upper, axis, up), lax.ppermute(lower, axis, down))  22.9 us
    pallas_call x1, Pallas kernels, solve_gain(): pl.pallas_call(solve_kernel, out_shape=jax.ShapeDtypeStruct(gain.shape, j...  21.9 us
    dot_general x4, matrix products, contract(): return lax.dot_general(a, b, (dims, ((), ())), precision=finest_accuracy)  4.15 us
  transfers between devices with their start and end apart: 7, of which 7 were waited for; matrix products, arithmetic and copies ran while one was open for 1% of the time, Pallas kernels for 13%

commit v1 on v0

v1 whole, which is shorter than its diff:
```python
import jax
import jax.numpy as jnp
from jax import lax
from jax.experimental import pallas as pl
from jax.experimental.pallas import tpu as pltpu
from jax.sharding import PartitionSpec as P

NC = 128
CYCLES = 2
TILE = 128
GROUP = 8


finest_accuracy = lax.Precision.HIGHEST


def from_everyone(array, axis):
    copies = jnp.broadcast_to(array, (lax.axis_size(axis), *array.shape))
    return lax.all_to_all(copies, axis, split_axis=0, concat_axis=0, tiled=True)


def from_neighbours(lower, upper, axis):
    size = lax.axis_size(axis)
    up = [(i, (i + 1) % size) for i in range(size)]
    down = [(j, i) for i, j in up]
    return lax.ppermute(upper, axis, up), lax.ppermute(lower, axis, down)


def stencil_weights(courant):
    return (
        courant * (1.0 + courant) * 0.5,
        1.0 - courant * courant,
        courant * (courant - 1.0) * 0.5,
    )


def sweep_local(field, courant, which_axis):
    weight_behind, weight_centre, weight_ahead = stencil_weights(courant)
    return (
        weight_behind * jnp.roll(field, 1, which_axis)
        + weight_centre * field
        + weight_ahead * jnp.roll(field, -1, which_axis)
    )


def sweep_padded(padded, courant, which_axis):
    keep = padded.shape[which_axis] - 2
    weight_behind, weight_centre, weight_ahead = stencil_weights(courant)
    return (
        weight_behind * lax.slice_in_dim(padded, 0, keep, axis=which_axis)
        + weight_centre * lax.slice_in_dim(padded, 1, keep + 1, axis=which_axis)
        + weight_ahead * lax.slice_in_dim(padded, 2, keep + 2, axis=which_axis)
    )


def wind_rows(courants, cycle, component, offset, length):
    surface = courants[cycle, component]
    doubled = jnp.concatenate([surface, surface], axis=0)
    return lax.dynamic_slice_in_dim(doubled, jnp.mod(offset, surface.shape[0]), length, 0)


def lane_spread(x, k):
    return jnp.broadcast_to(x[:, k : k + 1], x.shape)


def row_spread(x, k):
    return jnp.broadcast_to(x[k : k + 1, :], x.shape)


def tree_sum(terms):
    while len(terms) > 1:
        terms = [a + b for a, b in zip(terms[::2], terms[1::2])]
    return terms[0]


def inverse_tile(rows, lane, sub):
    rows = list(rows)
    for g in range(TILE // GROUP):
        panel = rows[g]
        first = GROUP * g
        inside = (lane >= first) & (lane < first + GROUP)
        cols = [lane_spread(panel, first + m) for m in range(GROUP)]
        for k in range(GROUP):
            here = sub == k
            flip = pl.reciprocal(row_spread(cols[k], k), approx=False)
            lead = cols[k]
            for m in range(GROUP):
                if m != k:
                    scaled = row_spread(cols[m], k) * flip
                    cols[m] = jnp.where(here, scaled, cols[m] - lead * scaled)
            cols[k] = jnp.where(here, flip, -lead * flip)
        panel = jnp.where(inside, jnp.where(lane - first == sub, 1.0, 0.0), panel)
        solved = tree_sum([cols[m] * row_spread(panel, m) for m in range(GROUP)])
        spread = [row_spread(solved, m) for m in range(GROUP)]
        for i in list(range(g + 1, len(rows))) + list(range(g)):
            change = tree_sum([lane_spread(rows[i], first + m) * spread[m] for m in range(GROUP)])
            rows[i] = jnp.where(inside, 0.0, rows[i]) - change
        rows[g] = solved
    return rows


def exact_dot(a, b):
    return jnp.dot(a, b, precision=finest_accuracy, preferred_element_type=jnp.float32)


def inverse_kernel(innovation_ref, noise_ref, out_ref):
    size = innovation_ref.shape[0]
    lane = lax.broadcasted_iota(jnp.int32, (GROUP, TILE), 1)
    sub = lax.broadcasted_iota(jnp.int32, (GROUP, TILE), 0)
    square = innovation_ref[...]
    square = 0.5 * (square + square.T)
    diagonal = lax.broadcasted_iota(jnp.int32, (size, size), 0) == lax.broadcasted_iota(
        jnp.int32, (size, size), 1
    )
    out_ref[...] = jnp.where(diagonal, square + noise_ref[...], square)
    tiles = size // TILE
    unit = jnp.where(
        lax.broadcasted_iota(jnp.int32, (TILE, TILE), 0)
        == lax.broadcasted_iota(jnp.int32, (TILE, TILE), 1),
        1.0,
        0.0,
    )

    def eliminate(t, carry):
        start = pl.multiple_of(t * TILE, TILE)
        here = pl.ds(start, TILE)
        rows = [
            out_ref[pl.ds(pl.multiple_of(start + GROUP * i, GROUP), GROUP), here]
            for i in range(TILE // GROUP)
        ]
        inverse = jnp.concatenate(inverse_tile(rows, lane, sub), axis=0)
        out_ref[here, here] = unit
        solved = exact_dot(inverse, out_ref[here, :])
        out_ref[here, :] = solved
        for other in range(1, tiles):
            there = pl.ds(pl.multiple_of(lax.rem(t + other, tiles) * TILE, TILE), TILE)
            column = out_ref[there, here]
            out_ref[there, here] = jnp.zeros((TILE, TILE), jnp.float32)
            out_ref[there, :] = out_ref[there, :] - exact_dot(column, solved)
        return carry

    lax.fori_loop(0, tiles, eliminate, 0)


def inverse_of(innovation, noise):
    return pl.pallas_call(
        inverse_kernel,
        out_shape=jax.ShapeDtypeStruct(innovation.shape, jnp.float32),
        in_specs=[pl.BlockSpec(memory_space=pltpu.VMEM)] * 2,
        out_specs=pl.BlockSpec(memory_space=pltpu.VMEM),
        name="inverse_of",
    )(innovation, noise[None, :])


def contract(a, b, dims):
    return lax.dot_general(a, b, (dims, ((), ())), precision=finest_accuracy)


def step_rows(field, courants, cycle, first):
    length = field.shape[0]
    field = sweep_local(field, wind_rows(courants, cycle, 0, first, length)[:, :, None], 1)
    north = wind_rows(courants, cycle, 1, first + 1, length - 2)[:, :, None]
    return sweep_padded(field, north, 0)


def step_columns(field, courants, cycle, first):
    length = field.shape[1]
    field = sweep_local(field, wind_rows(courants, cycle, 0, first, length)[None], 2)
    north = wind_rows(courants, cycle, 1, first + 1, length - 2)[None]
    return sweep_padded(field, north, 1)


def forecast_weights(targets, courants, first, length):
    cells = courants.shape[2] * NC
    span = length + 2 * CYCLES
    place = jnp.mod(targets - (first - CYCLES) * NC, cells)
    grid = lax.broadcasted_iota(jnp.int32, (1, span, NC), 1) * NC + lax.broadcasted_iota(
        jnp.int32, (1, span, NC), 2
    )
    weights = (place[:, None, None] == grid).astype(jnp.float32)
    for cycle in reversed(range(CYCLES)):
        size = weights.shape[1]
        origin = first - cycle - 1
        north = wind_rows(courants, cycle, 1, origin, size)[None]
        behind, centre, ahead = [w * weights for w in stencil_weights(north)]
        weights = behind[:, 2:] + centre[:, 1 : size - 1] + ahead[:, : size - 2]
        east = wind_rows(courants, cycle, 0, origin + 1, size - 2)[None]
        behind, centre, ahead = [w * weights for w in stencil_weights(east)]
        weights = jnp.roll(behind, -1, 2) + centre + jnp.roll(ahead, 1, 2)
    return weights.reshape(targets.shape[0], length * NC)


def three_bands(targets, band, share):
    doubled = jnp.concatenate([targets, targets])
    start = jnp.mod((band - 1) * share, targets.shape[0])
    return lax.dynamic_slice_in_dim(doubled, start, 3 * share)


def by_shifts(part, axis):
    size, mine = lax.axis_size(axis), lax.axis_index(axis)
    parts = jnp.zeros((size, *part.shape), part.dtype)
    parts = lax.dynamic_update_index_in_dim(parts, part, mine, 0)
    for shift in range(1, size):
        got = lax.ppermute(part, axis, [(i, (i + shift) % size) for i in range(size)])
        parts = lax.dynamic_update_index_in_dim(parts, got, jnp.mod(mine - shift, size), 0)
    return parts


def sum_of_bands(shares, axis):
    share = shares.shape[0] // 3
    from_below, from_above = from_neighbours(shares[:share], shares[2 * share :], axis)
    return shares[share : 2 * share] + from_below + from_above


def step_narrow(tile, courants, first, axis):
    edge, length = CYCLES * NC, tile.shape[1]
    before, after = from_neighbours(tile[:, :edge], tile[:, length - edge :], axis)
    field = jnp.concatenate([before, tile, after], axis=1).reshape(tile.shape[0], -1, NC)
    for cycle in range(CYCLES):
        field = step_columns(field, courants, cycle, first - CYCLES + cycle)
    return field.reshape(tile.shape)


def per_device(covariance, courants, process_noise_spread, sensor_targets, noise_variance):
    row_index, column_index = lax.axis_index(ROW), lax.axis_index(COL)
    height, width = covariance.shape
    band_rows, band_columns = height // NC, width // NC
    row_first, column_first = row_index * band_rows, column_index * band_columns
    edge = CYCLES * NC
    sensors = sensor_targets.shape[0]
    row_share = sensors // lax.axis_size(ROW)
    column_share = sensors // lax.axis_size(COL)
    row_targets = three_bands(sensor_targets, row_index, row_share)
    column_targets = three_bands(sensor_targets, column_index, column_share)
    row_sensors = row_targets[row_share : 2 * row_share]
    column_sensors = column_targets[column_share : 2 * column_share]
    row_ids = row_index * height + jnp.arange(height, dtype=jnp.int32)
    column_ids = column_index * width + jnp.arange(width, dtype=jnp.int32)
    noise_here = process_noise_spread.reshape(height, 1)
    pick_rows = row_sensors[:, None] == row_ids[None, :]
    pick_columns = column_sensors[:, None] == column_ids[None, :]
    row_noise = jnp.sum(jnp.where(pick_rows, noise_here[:, 0][None, :], 0.0), axis=1)

    with jax.named_scope("tiles"):
        row_weights = forecast_weights(row_targets, courants, row_first, band_rows)
        column_weights = forecast_weights(column_targets, courants, column_first, band_columns)
        obs = sum_of_bands(contract(row_weights, covariance, ((1,), (0,))), ROW)
        gain = sum_of_bands(contract(column_weights, covariance, ((1,), (1,))), COL)
        obs = step_narrow(obs, courants, column_first, COL)
        gain = step_narrow(gain, courants, row_first, ROW)
        obs = obs + jnp.where(
            row_sensors[:, None] == column_ids[None, :], row_noise[:, None], 0.0
        )
        gain = gain + jnp.where(
            column_sensors[:, None] == row_ids[None, :], noise_here[:, 0][None, :], 0.0
        )
        block = contract(obs, pick_columns.astype(jnp.float32), ((1,), (1,)))

    high = lax.axis_size("zh")
    with jax.named_scope("innovation"):
        block = from_everyone(block.reshape(-1, NC), ("y", "zl", "zh"))
        block, covariance, obs, gain = lax.optimization_barrier((block, covariance, obs, gain))
        block = block.reshape(-1, high, row_share, column_share)
        slab = block.transpose(1, 3, 0, 2).reshape(high * column_share, sensors)
        slabs = from_everyone(slab, ("x", "core"))
        flat = (lax.axis_size("x"), lax.axis_size("core"), high, column_share, sensors)
        innovation = slabs.reshape(flat).transpose(0, 2, 1, 3, 4).reshape(sensors, sensors)

    with jax.named_scope("forecast"):
        before, after = from_neighbours(covariance[:edge], covariance[height - edge :], ROW)
        field = jnp.concatenate([before, covariance, after], axis=0).reshape(-1, NC, width)
        for cycle in range(CYCLES):
            field = step_rows(field, courants, cycle, row_first - CYCLES + cycle)
        half_way = field.reshape(height, width)
        innovation, half_way = lax.optimization_barrier((innovation, half_way))
        before, after = from_neighbours(half_way[:, :edge], half_way[:, width - edge :], COL)
        inverse = inverse_of(innovation, noise_variance)

    with jax.named_scope("gathers"):
        obs_rows = by_shifts(obs, "zl").reshape(-1, width)
        gain = by_shifts(by_shifts(gain, "core"), "zh").reshape(-1, *gain.shape)
        gain = gain.reshape(-1, height)
        gain = by_shifts(gain, "x").reshape(sensors, height)
        obs_rows = from_everyone(obs_rows, "y").reshape(sensors, width)
        solved = contract(inverse, gain, ((1,), (0,)))

    with jax.named_scope("forecast_end"):
        field = jnp.concatenate([before, half_way, after], axis=1).reshape(height, -1, NC)
        for cycle in range(CYCLES):
            field = step_columns(field, courants, cycle, column_first - CYCLES + cycle)
        forecast = field.reshape(height, width) + jnp.where(
            row_ids[:, None] == column_ids[None, :], noise_here, 0.0
        )
    return forecast - contract(solved, obs_rows, ((0,), (0,)))


ROW = ("y", "zl")
COL = ("x", "zh", "core")


def physical(mesh):
    rows, columns = mesh.devices.shape
    zl, zh, core = 4, 2, 2
    shape = (rows // zl, zl, columns // (zh * core), zh, core)
    return jax.sharding.Mesh(mesh.devices.reshape(shape), ROW + COL)


def solution(mesh):
    in_specs = (P(ROW, COL), P(), P(ROW, None), P(), P())
    out_specs = P(ROW, COL)
    return jax.shard_map(
        per_device, mesh=physical(mesh), in_specs=in_specs, out_specs=out_specs, check_vma=False
    )
```

time: 168 us -> 191 us (1.14)
  the two profiles are of different devices: /device:TPU:16 before, /device:TPU:8 now
where the time goes in v1:
time: 191 us; the launch traced here: 190 us
  starting transfers between devices  112 us (59%)
  Pallas kernels  25.6 us (13%)
  waiting for transfers between devices  24 us (13%)
  local copies, waits for them, and re-layouts  11.9 us (6%)
  other arithmetic  9.65 us (5%)
  matrix products  5.3 us (3%)
    ppermute x12, starting transfers between devices, from_neighbours(): return (lax.ppermute(upper, axis, up), lax.ppermute(lower, axis, down))  63.9 us
    ppermute x8, starting transfers between devices, by_shifts(): lax.ppermute(part, axis, [(i, (i + shift) % size) for i in range(size)])  26.2 us
    pallas_call x1, Pallas kernels, inverse_of(): pl.pallas_call(inverse_kernel, out_shape=jax.ShapeDtypeStruct(innovation....  25.6 us
    all_to_all x3, starting transfers between devices, from_everyone(): return lax.all_to_all(copies, axis, split_axis=0, concat_axis=0, tiled=True)  22.4 us
    ppermute x8, waiting for transfers between devices, by_shifts(): lax.ppermute(part, axis, [(i, (i + shift) % size) for i in range(size)])  11.7 us
    all_to_all x3, waiting for transfers between devices, from_everyone(): return lax.all_to_all(copies, axis, split_axis=0, concat_axis=0, tiled=True)  11.3 us
    dot_general x5, matrix products, contract(): return lax.dot_general(a, b, (dims, ((), ())), precision=finest_accuracy)  5.3 us
  transfers between devices with their start and end apart: 23, of which 6 were waited for; matrix products, arithmetic and copies ran while one was open for 10% of the time, Pallas kernels for 13%

profile of v1, /device:TPU:8, one launch (start us, length us, event | category | flops | bytes accessed | tf_op | source)
XLA Modules:
  0.0 190.2 jit_solution(6050165683198166538)
XLA Ops:
  5.4 1.9 %collective-permute-start.4 = (f32[32,256]{1,0:T(8,128)S(1)}, f32[32,256]{1,0:T(8,128)S(1)}, u32[]{:S(2)}, u32[]{:S(2)}) collective-permute-start(f32[32,256]{1,0:T(8,128)S(1)} %get-tuple-element.77), channel_id=1, source_target_pairs={{0,1},{1,2},{2,3},{3,4},{4,5},{5,6},{6,7},{7,8},{8,9},{9,10},{10,1... | collective-permute-start | bytes 98312 | tf_op jit(solution)/shard_map/tiles/ppermute | solution.py:26
  7.3 12.6 %collective-permute-start.5 = (f32[32,256]{1,0:T(8,128)S(1)}, f32[32,256]{1,0:T(8,128)S(1)}, u32[]{:S(2)}, u32[]{:S(2)}) collective-permute-start(f32[32,256]{1,0:T(8,128)S(1)} %get-tuple-element.78), channel_id=1, source_target_pairs={{1,0},{2,1},{3,2},{4,3},{5,4},{6,5},{7,6},{8,7},{9,8},{10,9},{11,1... | collective-permute-start | bytes 98312 | tf_op jit(solution)/shard_map/tiles/ppermute | solution.py:26
  21.9 3.4 %collective-permute-start = (f32[16,512]{1,0:T(8,128)S(1)}, f32[16,512]{1,0:T(8,128)S(1)}, u32[]{:S(2)}, u32[]{:S(2)}) collective-permute-start(f32[16,512]{1,0:T(8,128)S(1)} %get-tuple-element.79), channel_id=1, source_target_pairs={{0,16},{16,32},{32,48},{48,64},{64,80},{80,96},{96,112},{112,128},... | collective-permute-start | bytes 98312 | tf_op jit(solution)/shard_map/tiles/ppermute | solution.py:26
  25.3 5.2 %collective-permute-start.1 = (f32[16,512]{1,0:T(8,128)S(1)}, f32[16,512]{1,0:T(8,128)S(1)}, u32[]{:S(2)}, u32[]{:S(2)}) collective-permute-start(f32[16,512]{1,0:T(8,128)S(1)} %get-tuple-element.80), channel_id=1, source_target_pairs={{16,0},{32,16},{48,32},{64,48},{80,64},{96,80},{112,96},{128,112},... | collective-permute-start | bytes 98312 | tf_op jit(solution)/shard_map/tiles/ppermute | solution.py:26
  32.1 1.9 %collective-permute-start.2 = (f32[16,256]{1,0:T(8,128)S(1)}, f32[16,256]{1,0:T(8,128)S(1)}, u32[]{:S(2)}, u32[]{:S(2)}) collective-permute-start(f32[16,256]{1,0:T(8,128)S(1)} %get-tuple-element.95), channel_id=1, source_target_pairs={{0,1},{1,2},{2,3},{3,4},{4,5},{5,6},{6,7},{7,8},{8,9},{9,10},{10,1... | collective-permute-start | bytes 49160 | tf_op jit(solution)/shard_map/tiles/ppermute | solution.py:26
  34.0 9.7 %collective-permute-start.3 = (f32[16,256]{1,0:T(8,128)S(1)}, f32[16,256]{1,0:T(8,128)S(1)}, u32[]{:S(2)}, u32[]{:S(2)}) collective-permute-start(f32[16,256]{1,0:T(8,128)S(1)} %get-tuple-element.96), channel_id=1, source_target_pairs={{1,0},{2,1},{3,2},{4,3},{5,4},{6,5},{7,6},{8,7},{9,8},{10,9},{11,1... | collective-permute-start | bytes 49160 | tf_op jit(solution)/shard_map/tiles/ppermute | solution.py:26
  43.7 2.4 %collective-permute-start.6 = (f32[32,256]{1,0:T(8,128)S(1)}, f32[32,256]{1,0:T(8,128)S(1)}, u32[]{:S(2)}, u32[]{:S(2)}) collective-permute-start(f32[32,256]{1,0:T(8,128)S(1)} %fusion.46), channel_id=1, source_target_pairs={{0,16},{16,32},{32,48},{48,64},{64,80},{80,96},{96,112},{112,128},... | collective-permute-start | bytes 98312 | tf_op jit(solution)/shard_map/tiles/ppermute | solution.py:26
  46.2 6.4 %collective-permute-start.7 = (f32[32,256]{1,0:T(8,128)S(1)}, f32[32,256]{1,0:T(8,128)S(1)}, u32[]{:S(2)}, u32[]{:S(2)}) collective-permute-start(f32[32,256]{1,0:T(8,128)S(1)} %fusion.46), channel_id=1, source_target_pairs={{16,0},{32,16},{48,32},{64,48},{80,64},{96,80},{112,96},{128,112},... | collective-permute-start | bytes 98312 | tf_op jit(solution)/shard_map/tiles/ppermute | solution.py:26
  54.3 11.9 %all-to-all-start = ((f32[64,4,128]{2,1,0:T(4,128)}), f32[64,4,128]{2,1,0:T(4,128)S(1)}, u32[]{:S(2)}, u32[]{:S(2)}) async-start(f32[64,4,128]{2,1,0:T(4,128)} %broadcast_in_dim.156), calls=%async_computation | async-start | bytes 262144 | tf_op jit(solution)/shard_map/innovation/all_to_all | solution.py:19
  67.2 11.3 %all-to-all-done = f32[64,4,128]{2,1,0:T(4,128)S(1)} async-done(((f32[64,4,128]{2,1,0:T(4,128)}), f32[64,4,128]{2,1,0:T(4,128)S(1)}, u32[]{:S(2)}, u32[]{:S(2)}) %all-to-all-start) | async-done | bytes 131104 | tf_op jit(solution)/shard_map/innovation/all_to_all | solution.py:19
  78.5 2.4 %collective-permute-start.8 = (f32[256,512]{1,0:T(8,128)S(1)}, f32[256,512]{1,0:T(8,128)S(1)}, u32[]{:S(2)}, u32[]{:S(2)}) collective-permute-start(f32[256,512]{1,0:T(8,128)S(1)} %copy-done), channel_id=1, source_target_pairs={{0,16},{16,32},{32,48},{48,64},{64,80},{80,96},{96,112},{112,128},... | collective-permute-start | bytes 1572872 | tf_op jit(solution)/shard_map/forecast/ppermute | solution.py:26
  80.8 6.2 %collective-permute-start.9 = (f32[256,512]{1,0:T(8,128)S(1)}, f32[256,512]{1,0:T(8,128)}, u32[]{:S(2)}, u32[]{:S(2)}) collective-permute-start(f32[256,512]{1,0:T(8,128)S(1)} %copy-done), channel_id=1, source_target_pairs={{16,0},{32,16},{48,32},{64,48},{80,64},{96,80},{112,96},{128,112},... | collective-permute-start | bytes 1572872 | tf_op jit(solution)/shard_map/forecast/ppermute | solution.py:26
  87.0 1.9 %collective-permute-start.17 = (f32[16,512]{1,0:T(8,128)S(1)}, f32[16,512]{1,0:T(8,128)S(1)}, u32[]{:S(2)}, u32[]{:S(2)}) collective-permute-start(f32[16,512]{1,0:T(8,128)S(1)} %bitcast_add_fusion.2), channel_id=1, source_target_pairs={{0,16},{16,32},{32,48},{48,0},{1,17},{17,33},{33,49},{49,1},{2,18}... | collective-permute-start | bytes 98312 | tf_op jit(solution)/shard_map/gathers/ppermute | solution.py:204
  88.9 1.9 %collective-permute-start.18 = (f32[16,512]{1,0:T(8,128)S(1)}, f32[16,512]{1,0:T(8,128)S(1)}, u32[]{:S(2)}, u32[]{:S(2)}) collective-permute-start(f32[16,512]{1,0:T(8,128)S(1)} %bitcast_add_fusion.2), channel_id=1, source_target_pairs={{0,32},{16,48},{32,0},{48,16},{1,33},{17,49},{33,1},{49,17},{2,34}... | collective-permute-start | bytes 98312 | tf_op jit(solution)/shard_map/gathers/ppermute | solution.py:204
  91.8 1.1 broadcast_in_dim.159
  92.9 4.4 %all-to-all-start.1 = ((f32[8,64,512]{2,1,0:T(8,128)}), f32[8,64,512]{2,1,0:T(8,128)S(1)}, u32[]{:S(2)}, u32[]{:S(2)}) async-start(f32[8,64,512]{2,1,0:T(8,128)} %broadcast_in_dim.159), calls=%async_computation.1 | async-start | bytes 2097152 | tf_op jit(solution)/shard_map/innovation/all_to_all | solution.py:19
  97.3 2.4 %collective-permute-start.12 = (f32[32,256]{1,0:T(8,128)S(1)}, f32[32,256]{1,0:T(8,128)S(1)}, u32[]{:S(2)}, u32[]{:S(2)}) collective-permute-start(f32[32,256]{1,0:T(8,128)S(1)} %bitcast_add_fusion.1), channel_id=1, source_target_pairs={{0,1},{1,0},{2,3},{3,2},{4,5},{5,4},{6,7},{7,6},{8,9},{9,8},{10,11... | collective-permute-start | bytes 98312 | tf_op jit(solution)/shard_map/gathers/ppermute | solution.py:204
  100.5 5.7 %collective-permute-start.19 = (f32[16,512]{1,0:T(8,128)S(1)}, f32[16,512]{1,0:T(8,128)S(1)}, u32[]{:S(2)}, u32[]{:S(2)}) collective-permute-start(f32[16,512]{1,0:T(8,128)S(1)} %bitcast_add_fusion.2), channel_id=1, source_target_pairs={{0,48},{16,0},{32,16},{48,32},{1,49},{17,1},{33,17},{49,33},{2,50}... | collective-permute-start | bytes 98312 | tf_op jit(solution)/shard_map/gathers/ppermute | solution.py:204
  106.3 2.5 %collective-permute-start.13 = (f32[2,32,256]{2,1,0:T(8,128)S(1)}, f32[2,32,256]{2,1,0:T(8,128)S(1)}, u32[]{:S(2)}, u32[]{:S(2)}) collective-permute-start(f32[2,32,256]{2,1,0:T(8,128)S(1)} %bitcast_dynamic-update-slice_fusion.9), channel_id=1, source_target_pairs={{0,2},{2,0},{1,3},{3,1},{4,6},{6,4},{5,7},{7,5},{8,10},{10,8},{9,1... | collective-permute-start | bytes 196616 | tf_op jit(solution)/shard_map/gathers/ppermute | solution.py:204
  108.8 7.5 %collective-permute-done.13 = f32[2,32,256]{2,1,0:T(8,128)S(1)} collective-permute-done((f32[2,32,256]{2,1,0:T(8,128)S(1)}, f32[2,32,256]{2,1,0:T(8,128)S(1)}, u32[]{:S(2)}, u32[]{:S(2)}) %collective-permute-start.13) | collective-permute-done | bytes 65568 | tf_op jit(solution)/shard_map/gathers/ppermute | solution.py:204
  116.4 3.8 %collective-permute-start.14 = (f32[128,256]{1,0:T(8,128)S(1)}, f32[128,256]{1,0:T(8,128)S(1)}, u32[]{:S(2)}, u32[]{:S(2)}) collective-permute-start(f32[128,256]{1,0:T(8,128)S(1)} %bitcast.120), channel_id=1, source_target_pairs={{0,4},{4,8},{8,12},{12,0},{1,5},{5,9},{9,13},{13,1},{2,6},{6,10},{... | collective-permute-start | bytes 393224 | tf_op jit(solution)/shard_map/gathers/ppermute | solution.py:204
  120.2 4.6 %collective-permute-start.15 = (f32[128,256]{1,0:T(8,128)S(1)}, f32[128,256]{1,0:T(8,128)S(1)}, u32[]{:S(2)}, u32[]{:S(2)}) collective-permute-start(f32[128,256]{1,0:T(8,128)S(1)} %bitcast.121), channel_id=1, source_target_pairs={{0,8},{4,12},{8,0},{12,4},{1,9},{5,13},{9,1},{13,5},{2,10},{6,14},... | collective-permute-start | bytes 393224 | tf_op jit(solution)/shard_map/gathers/ppermute | solution.py:204
  124.8 3.4 %collective-permute-start.16 = (f32[128,256]{1,0:T(8,128)S(1)}, f32[128,256]{1,0:T(8,128)S(1)}, u32[]{:S(2)}, u32[]{:S(2)}) collective-permute-start(f32[128,256]{1,0:T(8,128)S(1)} %bitcast.122), channel_id=1, source_target_pairs={{0,12},{4,0},{8,4},{12,8},{1,13},{5,1},{9,5},{13,9},{2,14},{6,2},{... | collective-permute-start | bytes 393224 | tf_op jit(solution)/shard_map/gathers/ppermute | solution.py:204
  128.6 3.1 %collective-permute-done.16 = f32[128,256]{1,0:T(8,128)S(1)} collective-permute-done((f32[128,256]{1,0:T(8,128)S(1)}, f32[128,256]{1,0:T(8,128)S(1)}, u32[]{:S(2)}, u32[]{:S(2)}) %collective-permute-start.16) | collective-permute-done | bytes 131104 | tf_op jit(solution)/shard_map/gathers/ppermute | solution.py:204
  131.7 1.3 pad_maximum_fusion
  135.4 1.1 broadcast_in_dim.179
  136.6 6.1 %all-to-all-start.2 = ((f32[8,64,512]{2,1,0:T(8,128)}), f32[8,64,512]{2,1,0:T(8,128)S(1)}, u32[]{:S(2)}, u32[]{:S(2)}) async-start(f32[8,64,512]{2,1,0:T(8,128)} %broadcast_in_dim.179), calls=%async_computation.2 | async-start | bytes 2097152 | tf_op jit(solution)/shard_map/gathers/all_to_all | solution.py:19
  143.8 2.1 %collective-permute-start.10 = (f32[256,256]{1,0:T(8,128)S(1)}, f32[256,256]{1,0:T(8,128)S(1)}, u32[]{:S(2)}, u32[]{:S(2)}) collective-permute-start(f32[256,256]{1,0:T(8,128)S(1)} %get-tuple-element.65), channel_id=1, source_target_pairs={{0,1},{1,2},{2,3},{3,4},{4,5},{5,6},{6,7},{7,8},{8,9},{9,10},{10,1... | collective-permute-start | bytes 786440 | tf_op jit(solution)/shard_map/forecast/ppermute | solution.py:26
  145.9 9.8 %collective-permute-start.11 = (f32[256,256]{1,0:T(8,128)S(1)}, f32[256,256]{1,0:T(8,128)}, u32[]{:S(2)}, u32[]{:S(2)}) collective-permute-start(f32[256,256]{1,0:T(8,128)S(1)} %get-tuple-element.66), channel_id=1, source_target_pairs={{1,0},{2,1},{3,2},{4,3},{5,4},{6,5},{7,6},{8,7},{9,8},{10,9},{11,1... | collective-permute-start | bytes 786440 | tf_op jit(solution)/shard_map/forecast/ppermute | solution.py:26
  155.7 25.6 %inverse_of.1 = f32[512,512]{1,0:T(8,128)} custom-call(f32[512,512]{1,0:T(8,128)} %bitcast.103, f32[1,512]{1,0:T(1,128)} %bitcast.138), custom_call_target="tpu_custom_call" | custom-call | tf_op jit(solution)/shard_map/forecast/inverse_of/pallas_call | solution.py:146
  181.3 2.2 %fusion.124 = f32[512,256]{1,0:T(8,128)S(1)} fusion(f32[512,512]{1,0:T(8,128)} %inverse_of.1, f32[512,256]{1,0:T(8,128)S(1)} %bitcast.111), kind=kOutput, calls=%fused_computation.273 | convolution fusion | flops 805306368 | bytes 2097152 | tf_op jit(solution)/shard_map/gathers/dot_general | solution.py:156
  188.3 1.9 convolution_subtract_fusion
  (169 shorter events, 21.3 us)
Async XLA Ops:
  3.7 1.0 copy-start
  5.4 38.3 %collective-permute-start.4 = (f32[32,256]{1,0:T(8,128)S(1)}, f32[32,256]{1,0:T(8,128)S(1)}, u32[]{:S(2)}, u32[]{:S(2)}) collective-permute-start(f32[32,256]{1,0:T(8,128)S(1)} %get-tuple-element.77), channel_id=1, source_target_pairs={{0,1},{1,2},{2,3},{3,4},{4,5},{5,6},{6,7},{7,8},{8,9},{9,10},{10,1... | collective-permute-start | bytes 98312 | tf_op jit(solution)/shard_map/tiles/ppermute | solution.py:26
  7.3 36.4 %collective-permute-start.5 = (f32[32,256]{1,0:T(8,128)S(1)}, f32[32,256]{1,0:T(8,128)S(1)}, u32[]{:S(2)}, u32[]{:S(2)}) collective-permute-start(f32[32,256]{1,0:T(8,128)S(1)} %get-tuple-element.78), channel_id=1, source_target_pairs={{1,0},{2,1},{3,2},{4,3},{5,4},{6,5},{7,6},{8,7},{9,8},{10,9},{11,1... | collective-permute-start | bytes 98312 | tf_op jit(solution)/shard_map/tiles/ppermute | solution.py:26
  20.2 10.4 %copy-start.3 = (f32[2,128]{1,0:T(2,128)S(1)}, f32[2,128]{1,0:T(2,128)}, u32[]{:S(2)}) copy-start(f32[2,128]{1,0:T(2,128)} %param.7) | copy-start | bytes 3076
  21.9 9.2 %collective-permute-start = (f32[16,512]{1,0:T(8,128)S(1)}, f32[16,512]{1,0:T(8,128)S(1)}, u32[]{:S(2)}, u32[]{:S(2)}) collective-permute-start(f32[16,512]{1,0:T(8,128)S(1)} %get-tuple-element.79), channel_id=1, source_target_pairs={{0,16},{16,32},{32,48},{48,64},{64,80},{80,96},{96,112},{112,128},... | collective-permute-start | bytes 98312 | tf_op jit(solution)/shard_map/tiles/ppermute | solution.py:26
  25.3 6.7 %collective-permute-start.1 = (f32[16,512]{1,0:T(8,128)S(1)}, f32[16,512]{1,0:T(8,128)S(1)}, u32[]{:S(2)}, u32[]{:S(2)}) collective-permute-start(f32[16,512]{1,0:T(8,128)S(1)} %get-tuple-element.80), channel_id=1, source_target_pairs={{16,0},{32,16},{48,32},{64,48},{80,64},{96,80},{112,96},{128,112},... | collective-permute-start | bytes 98312 | tf_op jit(solution)/shard_map/tiles/ppermute | solution.py:26
  32.1 20.5 %collective-permute-start.2 = (f32[16,256]{1,0:T(8,128)S(1)}, f32[16,256]{1,0:T(8,128)S(1)}, u32[]{:S(2)}, u32[]{:S(2)}) collective-permute-start(f32[16,256]{1,0:T(8,128)S(1)} %get-tuple-element.95), channel_id=1, source_target_pairs={{0,1},{1,2},{2,3},{3,4},{4,5},{5,6},{6,7},{7,8},{8,9},{9,10},{10,1... | collective-permute-start | bytes 49160 | tf_op jit(solution)/shard_map/tiles/ppermute | solution.py:26
  34.0 18.6 %collective-permute-start.3 = (f32[16,256]{1,0:T(8,128)S(1)}, f32[16,256]{1,0:T(8,128)S(1)}, u32[]{:S(2)}, u32[]{:S(2)}) collective-permute-start(f32[16,256]{1,0:T(8,128)S(1)} %get-tuple-element.96), channel_id=1, source_target_pairs={{1,0},{2,1},{3,2},{4,3},{5,4},{6,5},{7,6},{8,7},{9,8},{10,9},{11,1... | collective-permute-start | bytes 49160 | tf_op jit(solution)/shard_map/tiles/ppermute | solution.py:26
  43.7 22.5 %collective-permute-start.6 = (f32[32,256]{1,0:T(8,128)S(1)}, f32[32,256]{1,0:T(8,128)S(1)}, u32[]{:S(2)}, u32[]{:S(2)}) collective-permute-start(f32[32,256]{1,0:T(8,128)S(1)} %fusion.46), channel_id=1, source_target_pairs={{0,16},{16,32},{32,48},{48,64},{64,80},{80,96},{96,112},{112,128},... | collective-permute-start | bytes 98312 | tf_op jit(solution)/shard_map/tiles/ppermute | solution.py:26
  46.2 20.1 %collective-permute-start.7 = (f32[32,256]{1,0:T(8,128)S(1)}, f32[32,256]{1,0:T(8,128)S(1)}, u32[]{:S(2)}, u32[]{:S(2)}) collective-permute-start(f32[32,256]{1,0:T(8,128)S(1)} %fusion.46), channel_id=1, source_target_pairs={{16,0},{32,16},{48,32},{64,48},{80,64},{96,80},{112,96},{128,112},... | collective-permute-start | bytes 98312 | tf_op jit(solution)/shard_map/tiles/ppermute | solution.py:26
  54.3 24.1 %all-to-all-start = ((f32[64,4,128]{2,1,0:T(4,128)}), f32[64,4,128]{2,1,0:T(4,128)S(1)}, u32[]{:S(2)}, u32[]{:S(2)}) async-start(f32[64,4,128]{2,1,0:T(4,128)} %broadcast_in_dim.156), calls=%async_computation | async-start | bytes 262144 | tf_op jit(solution)/shard_map/innovation/all_to_all | solution.py:19
  78.5 53.2 %collective-permute-start.8 = (f32[256,512]{1,0:T(8,128)S(1)}, f32[256,512]{1,0:T(8,128)S(1)}, u32[]{:S(2)}, u32[]{:S(2)}) collective-permute-start(f32[256,512]{1,0:T(8,128)S(1)} %copy-done), channel_id=1, source_target_pairs={{0,16},{16,32},{32,48},{48,64},{64,80},{80,96},{96,112},{112,128},... | collective-permute-start | bytes 1572872 | tf_op jit(solution)/shard_map/forecast/ppermute | solution.py:26
  80.8 50.8 %collective-permute-start.9 = (f32[256,512]{1,0:T(8,128)S(1)}, f32[256,512]{1,0:T(8,128)}, u32[]{:S(2)}, u32[]{:S(2)}) collective-permute-start(f32[256,512]{1,0:T(8,128)S(1)} %copy-done), channel_id=1, source_target_pairs={{16,0},{32,16},{48,32},{64,48},{80,64},{96,80},{112,96},{128,112},... | collective-permute-start | bytes 1572872 | tf_op jit(solution)/shard_map/forecast/ppermute | solution.py:26
  87.0 19.3 %collective-permute-start.17 = (f32[16,512]{1,0:T(8,128)S(1)}, f32[16,512]{1,0:T(8,128)S(1)}, u32[]{:S(2)}, u32[]{:S(2)}) collective-permute-start(f32[16,512]{1,0:T(8,128)S(1)} %bitcast_add_fusion.2), channel_id=1, source_target_pairs={{0,16},{16,32},{32,48},{48,0},{1,17},{17,33},{33,49},{49,1},{2,18}... | collective-permute-start | bytes 98312 | tf_op jit(solution)/shard_map/gathers/ppermute | solution.py:204
  88.9 19.9 %collective-permute-start.18 = (f32[16,512]{1,0:T(8,128)S(1)}, f32[16,512]{1,0:T(8,128)S(1)}, u32[]{:S(2)}, u32[]{:S(2)}) collective-permute-start(f32[16,512]{1,0:T(8,128)S(1)} %bitcast_add_fusion.2), channel_id=1, source_target_pairs={{0,32},{16,48},{32,0},{48,16},{1,33},{17,49},{33,1},{49,17},{2,34}... | collective-permute-start | bytes 98312 | tf_op jit(solution)/shard_map/gathers/ppermute | solution.py:204
  92.9 42.5 %all-to-all-start.1 = ((f32[8,64,512]{2,1,0:T(8,128)}), f32[8,64,512]{2,1,0:T(8,128)S(1)}, u32[]{:S(2)}, u32[]{:S(2)}) async-start(f32[8,64,512]{2,1,0:T(8,128)} %broadcast_in_dim.159), calls=%async_computation.1 | async-start | bytes 2097152 | tf_op jit(solution)/shard_map/innovation/all_to_all | solution.py:19
  97.3 3.2 %collective-permute-start.12 = (f32[32,256]{1,0:T(8,128)S(1)}, f32[32,256]{1,0:T(8,128)S(1)}, u32[]{:S(2)}, u32[]{:S(2)}) collective-permute-start(f32[32,256]{1,0:T(8,128)S(1)} %bitcast_add_fusion.1), channel_id=1, source_target_pairs={{0,1},{1,0},{2,3},{3,2},{4,5},{5,4},{6,7},{7,6},{8,9},{9,8},{10,11... | collective-permute-start | bytes 98312 | tf_op jit(solution)/shard_map/gathers/ppermute | solution.py:204
  100.5 19.7 %collective-permute-start.19 = (f32[16,512]{1,0:T(8,128)S(1)}, f32[16,512]{1,0:T(8,128)S(1)}, u32[]{:S(2)}, u32[]{:S(2)}) collective-permute-start(f32[16,512]{1,0:T(8,128)S(1)} %bitcast_add_fusion.2), channel_id=1, source_target_pairs={{0,48},{16,0},{32,16},{48,32},{1,49},{17,1},{33,17},{49,33},{2,50}... | collective-permute-start | bytes 98312 | tf_op jit(solution)/shard_map/gathers/ppermute | solution.py:204
  106.3 10.1 %collective-permute-start.13 = (f32[2,32,256]{2,1,0:T(8,128)S(1)}, f32[2,32,256]{2,1,0:T(8,128)S(1)}, u32[]{:S(2)}, u32[]{:S(2)}) collective-permute-start(f32[2,32,256]{2,1,0:T(8,128)S(1)} %bitcast_dynamic-update-slice_fusion.9), channel_id=1, source_target_pairs={{0,2},{2,0},{1,3},{3,1},{4,6},{6,4},{5,7},{7,5},{8,10},{10,8},{9,1... | collective-permute-start | bytes 196616 | tf_op jit(solution)/shard_map/gathers/ppermute | solution.py:204
  116.4 11.8 %collective-permute-start.14 = (f32[128,256]{1,0:T(8,128)S(1)}, f32[128,256]{1,0:T(8,128)S(1)}, u32[]{:S(2)}, u32[]{:S(2)}) collective-permute-start(f32[128,256]{1,0:T(8,128)S(1)} %bitcast.120), channel_id=1, source_target_pairs={{0,4},{4,8},{8,12},{12,0},{1,5},{5,9},{9,13},{13,1},{2,6},{6,10},{... | collective-permute-start | bytes 393224 | tf_op jit(solution)/shard_map/gathers/ppermute | solution.py:204
  120.2 8.4 %collective-permute-start.15 = (f32[128,256]{1,0:T(8,128)S(1)}, f32[128,256]{1,0:T(8,128)S(1)}, u32[]{:S(2)}, u32[]{:S(2)}) collective-permute-start(f32[128,256]{1,0:T(8,128)S(1)} %bitcast.121), channel_id=1, source_target_pairs={{0,8},{4,12},{8,0},{12,4},{1,9},{5,13},{9,1},{13,5},{2,10},{6,14},... | collective-permute-start | bytes 393224 | tf_op jit(solution)/shard_map/gathers/ppermute | solution.py:204
  124.8 6.9 %collective-permute-start.16 = (f32[128,256]{1,0:T(8,128)S(1)}, f32[128,256]{1,0:T(8,128)S(1)}, u32[]{:S(2)}, u32[]{:S(2)}) collective-permute-start(f32[128,256]{1,0:T(8,128)S(1)} %bitcast.122), channel_id=1, source_target_pairs={{0,12},{4,0},{8,4},{12,8},{1,13},{5,1},{9,5},{13,9},{2,14},{6,2},{... | collective-permute-start | bytes 393224 | tf_op jit(solution)/shard_map/gathers/ppermute | solution.py:204
  131.7 1.4 copy-start.1
  136.6 51.8 %all-to-all-start.2 = ((f32[8,64,512]{2,1,0:T(8,128)}), f32[8,64,512]{2,1,0:T(8,128)S(1)}, u32[]{:S(2)}, u32[]{:S(2)}) async-start(f32[8,64,512]{2,1,0:T(8,128)} %broadcast_in_dim.179), calls=%async_computation.2 | async-start | bytes 2097152 | tf_op jit(solution)/shard_map/gathers/all_to_all | solution.py:19
  143.8 37.5 %copy-start.2 = (f32[4,128,256]{2,1,0:T(8,128)S(1)}, f32[4,128,256]{2,1,0:T(8,128)}, u32[]{:S(2)}) copy-start(f32[4,128,256]{2,1,0:T(8,128)} %copy-done.1) | copy-start | bytes 1572868
  143.8 39.7 %collective-permute-start.10 = (f32[256,256]{1,0:T(8,128)S(1)}, f32[256,256]{1,0:T(8,128)S(1)}, u32[]{:S(2)}, u32[]{:S(2)}) collective-permute-start(f32[256,256]{1,0:T(8,128)S(1)} %get-tuple-element.65), channel_id=1, source_target_pairs={{0,1},{1,2},{2,3},{3,4},{4,5},{5,6},{6,7},{7,8},{8,9},{9,10},{10,1... | collective-permute-start | bytes 786440 | tf_op jit(solution)/shard_map/forecast/ppermute | solution.py:26
  145.9 37.7 %collective-permute-start.11 = (f32[256,256]{1,0:T(8,128)S(1)}, f32[256,256]{1,0:T(8,128)}, u32[]{:S(2)}, u32[]{:S(2)}) collective-permute-start(f32[256,256]{1,0:T(8,128)S(1)} %get-tuple-element.66), channel_id=1, source_target_pairs={{1,0},{2,1},{3,2},{4,3},{5,4},{6,5},{7,6},{8,7},{9,8},{10,9},{11,1... | collective-permute-start | bytes 786440 | tf_op jit(solution)/shard_map/forecast/ppermute | solution.py:26

commit v2 on v0

--- a/solution.py
+++ b/solution.py
@@ -103,7 +103,7 @@
     return jnp.dot(a, b, precision=finest_accuracy, preferred_element_type=jnp.float32)
 
 
-def solve_kernel(innovation_ref, noise_ref, gain_ref, out_ref, work):
+def inverse_kernel(innovation_ref, noise_ref, out_ref):
     size = innovation_ref.shape[0]
     lane = lax.broadcasted_iota(jnp.int32, (GROUP, TILE), 1)
     sub = lax.broadcasted_iota(jnp.int32, (GROUP, TILE), 0)
@@ -112,66 +112,86 @@
     diagonal = lax.broadcasted_iota(jnp.int32, (size, size), 0) == lax.broadcasted_iota(
         jnp.int32, (size, size), 1
     )
-    work[:, :size] = jnp.where(diagonal, square + noise_ref[...], square)
-    work[:, size:] = gain_ref[...]
+    out_ref[...] = jnp.where(diagonal, square + noise_ref[...], square)
     tiles = size // TILE
+    spans = [slice(t * TILE, (t + 1) * TILE) for t in range(tiles)]
     for t in range(tiles):
-        lo, hi = t * TILE, (t + 1) * TILE
-        rows = [work[lo + GROUP * i : lo + GROUP * (i + 1), lo:hi] for i in range(TILE // GROUP)]
+        here = spans[t]
+        rows = [
+            out_ref[t * TILE + GROUP * i : t * TILE + GROUP * (i + 1), here]
+            for i in range(TILE // GROUP)
+        ]
         inverse = jnp.concatenate(inverse_tile(rows, lane, sub), axis=0)
-        solved = exact_dot(inverse, work[lo:hi, hi:])
+        for j in range(tiles):
+            if j != t:
+                out_ref[here, spans[j]] = exact_dot(inverse, out_ref[here, spans[j]])
         for i in range(tiles):
             if i != t:
-                span = slice(i * TILE, (i + 1) * TILE)
-                work[span, hi:] = work[span, hi:] - exact_dot(work[span, lo:hi], solved)
-        work[lo:hi, hi:] = solved
-    out_ref[...] = work[:, size:]
-
-
-def solve_gain(innovation, noise, gain):
+                column = out_ref[spans[i], here]
+                for j in range(tiles):
+                    if j != t:
+                        out_ref[spans[i], spans[j]] = out_ref[spans[i], spans[j]] - exact_dot(
+                            column, out_ref[here, spans[j]]
+                        )
+                out_ref[spans[i], here] = -exact_dot(column, inverse)
+        out_ref[here, here] = inverse
+
+
+def inverse_of(innovation, noise):
     return pl.pallas_call(
-        solve_kernel,
-        out_shape=jax.ShapeDtypeStruct(gain.shape, jnp.float32),
-        in_specs=[pl.BlockSpec(memory_space=pltpu.VMEM)] * 3,
+        inverse_kernel,
+        out_shape=jax.ShapeDtypeStruct(innovation.shape, jnp.float32),
+        in_specs=[pl.BlockSpec(memory_space=pltpu.VMEM)] * 2,
         out_specs=pl.BlockSpec(memory_space=pltpu.VMEM),
-        scratch_shapes=[pltpu.VMEM((gain.shape[0], gain.shape[0] + gain.shape[1]), jnp.float32)],
-        name="solve_gain",
-    )(innovation, noise[None, :], gain)
+        name="inverse_of",
+    )(innovation, noise[None, :])
 
 
 def contract(a, b, dims):
     return lax.dot_general(a, b, (dims, ((), ())), precision=finest_accuracy)
 
 
-def per_device(covariance, courants, process_noise_spread, sensor_targets, noise_variance):
-    row_index = lax.axis_index("row")
-    column_index = lax.axis_index("col")
+def step_rows(field, courants, cycle, first):
+    length = field.shape[0]
+    field = sweep_local(field, wind_rows(courants, cycle, 0, first, length)[:, :, None], 1)
+    north = wind_rows(courants, cycle, 1, first + 1, length - 2)[:, :, None]
+    return sweep_padded(field, north, 0)
+
+
+def step_columns(field, courants, cycle, first):
+    length = field.shape[1]
+    field = sweep_local(field, wind_rows(courants, cycle, 0, first, length)[None], 2)
+    north = wind_rows(courants, cycle, 1, first + 1, length - 2)[None]
+    return sweep_padded(field, north, 1)
+
+
+def by_shifts(part, axis):
+    size, mine = lax.axis_size(axis), lax.axis_index(axis)
+    parts = jnp.zeros((size, *part.shape), part.dtype)
+    parts = lax.dynamic_update_index_in_dim(parts, part, mine, 0)
+    for shift in range(1, size):
+        got = lax.ppermute(part, axis, [(i, (i + shift) % size) for i in range(size)])
+        parts = lax.dynamic_update_index_in_dim(parts, got, jnp.mod(mine - shift, size), 0)
+    return parts
+
+
+def one_cycle(covariance, courants, process_noise_spread, sensor_targets, noise_variance):
+    row_index, column_index = lax.axis_index(ROW), lax.axis_index(COL)
     height, width = covariance.shape
     band_rows, band_columns = height // NC, width // NC
     row_first, column_first = row_index * band_rows, column_index * band_columns
-
-    before, after = from_neighbours(
-        covariance[: CYCLES * NC], covariance[height - CYCLES * NC :], "row"
-    )
+    edge = CYCLES * NC
+
+    before, after = from_neighbours(covariance[:edge], covariance[height - edge :], ROW)
     field = jnp.concatenate([before, covariance, after], axis=0).reshape(-1, NC, width)
     for cycle in range(CYCLES):
-        length = field.shape[0]
-        offset = row_first - (CYCLES - cycle)
-        field = sweep_local(field, wind_rows(courants, cycle, 0, offset, length)[:, :, None], 1)
-        north = wind_rows(courants, cycle, 1, offset + 1, length - 2)[:, :, None]
-        field = sweep_padded(field, north, 0)
+        field = step_rows(field, courants, cycle, row_first - CYCLES + cycle)
     half_way = field.reshape(height, width)
 
-    before, after = from_neighbours(
-        half_way[:, : CYCLES * NC], half_way[:, width - CYCLES * NC :], "col"
-    )
+    before, after = from_neighbours(half_way[:, :edge], half_way[:, width - edge :], COL)
     field = jnp.concatenate([before, half_way, after], axis=1).reshape(height, -1, NC)
     for cycle in range(CYCLES):
-        length = field.shape[1]
-        offset = column_first - (CYCLES - cycle)
-        field = sweep_local(field, wind_rows(courants, cycle, 0, offset, length)[None], 2)
-        north = wind_rows(courants, cycle, 1, offset + 1, length - 2)[None]
-        field = sweep_padded(field, north, 1)
+        field = step_columns(field, courants, cycle, column_first - CYCLES + cycle)
     forecast = field.reshape(height, width)
 
     row_ids = row_index * height + jnp.arange(height, dtype=jnp.int32)
@@ -181,28 +201,49 @@
     )
 
     sensors = sensor_targets.shape[0]
-    row_share = sensors // lax.axis_size("row")
-    column_share = sensors // lax.axis_size("col")
+    row_share = sensors // lax.axis_size(ROW)
+    column_share = sensors // lax.axis_size(COL)
     row_sensors = lax.dynamic_slice_in_dim(sensor_targets, row_index * row_share, row_share)
     column_sensors = lax.dynamic_slice_in_dim(
         sensor_targets, column_index * column_share, column_share
     )
     pick_rows = (row_sensors[:, None] == row_ids[None, :]).astype(jnp.float32)
     pick_columns = (column_sensors[:, None] == column_ids[None, :]).astype(jnp.float32)
-
-    gain = from_everyone(contract(pick_columns, forecast, ((1,), (1,))), "col")
-    gain = gain.reshape(sensors, height)
-    strip = contract(pick_rows, gain, ((1,), (1,)))
-    innovation = from_everyone(strip, "row").reshape(sensors, sensors)
-    obs_rows = from_everyone(contract(pick_rows, forecast, ((1,), (0,))), "row")
-    obs_rows = obs_rows.reshape(sensors, width)
-    solved = solve_gain(innovation, noise_variance, gain)
+    obs = contract(pick_rows, forecast, ((1,), (0,)))
+    block = contract(obs, pick_columns, ((1,), (1,)))
+    gain = contract(pick_columns, forecast, ((1,), (1,)))
+
+    high = lax.axis_size("zh")
+    block = from_everyone(block.reshape(-1, NC), ("y", "zl", "zh"))
+    gain = by_shifts(by_shifts(gain, "core"), "zh").reshape(-1, height)
+    block, gain, obs = lax.optimization_barrier((block, gain, obs))
+    block = block.reshape(-1, high, row_share, column_share)
+    slab = block.transpose(1, 3, 0, 2).reshape(high * column_share, sensors)
+    slabs = from_everyone(slab, ("x", "core"))
+    flat = (lax.axis_size("x"), lax.axis_size("core"), high, column_share, sensors)
+    innovation = slabs.reshape(flat).transpose(0, 2, 1, 3, 4).reshape(sensors, sensors)
+
+    gain = by_shifts(gain, "x").reshape(sensors, height)
+    innovation, gain, obs = lax.optimization_barrier((innovation, gain, obs))
+    obs_rows = from_everyone(obs, ROW).reshape(sensors, width)
+    solved = contract(inverse_of(innovation, noise_variance), gain, ((1,), (0,)))
     return forecast - contract(solved, obs_rows, ((0,), (0,)))
 
 
+ROW = ("y", "zl")
+COL = ("x", "zh", "core")
+
+
+def physical(mesh):
+    rows, columns = mesh.devices.shape
+    zl, zh, core = 4, 2, 2
+    shape = (rows // zl, zl, columns // (zh * core), zh, core)
+    return jax.sharding.Mesh(mesh.devices.reshape(shape), ROW + COL)
+
+
 def solution(mesh):
-    in_specs = (P("row", "col"), P(), P("row", None), P(), P())
-    out_specs = P("row", "col")
+    in_specs = (P(ROW, COL), P(), P(ROW, None), P(), P())
+    out_specs = P(ROW, COL)
     return jax.shard_map(
-        per_device, mesh=mesh, in_specs=in_specs, out_specs=out_specs, check_vma=False
-    )
+        one_cycle, mesh=physical(mesh), in_specs=in_specs, out_specs=out_specs, check_vma=False
+    )

time: 168 us -> 165 us (0.982)
  waiting for transfers between devices: 76 us -> 49.8 us
  starting transfers between devices: 52.3 us -> 72.3 us
  local copies, waits for them, and re-layouts: 6.91 us -> 8.71 us
    all_to_all x3, waiting for transfers between devices: 49.3 us -> 19.8 us  [from_everyone(): return lax.all_to_all(copies, axis, split_axis=0, concat_axis=0, tiled=True)]
    ppermute x0 -> x5, starting transfers between devices: none -> 25 us  [by_shifts(): lax.ppermute(part, axis, [(i, (i + shift) % size) for i in range(size)])]
    all_to_all x3, starting transfers between devices: 29.4 us -> 24.4 us  [from_everyone(): return lax.all_to_all(copies, axis, split_axis=0, concat_axis=0, tiled=True)]
    ppermute x0 -> x5, waiting for transfers between devices: none -> 3.43 us  [by_shifts(): lax.ppermute(part, axis, [(i, (i + shift) % size) for i in range(size)])]
    dot_general x4 -> x5, matrix products: 4.15 us -> 5.16 us  [contract(): return lax.dot_general(a, b, (dims, ((), ())), precision=finest_accuracy)]
  transfers between devices with their start and end apart: 7 -> 12, of which waited for: 7 -> 8; matrix products, arithmetic and copies ran while one was open for 1% -> 4% of each run, Pallas kernels for 13% -> 13%
where the time goes in v2:
time: 165 us; the launch traced here: 164 us
  starting transfers between devices  72.3 us (44%)
  waiting for transfers between devices  49.8 us (30%)
  Pallas kernels  22.1 us (13%)
  local copies, waits for them, and re-layouts  8.71 us (5%)
  other arithmetic  5.27 us (3%)
  matrix products  5.16 us (3%)
    ppermute x4, waiting for transfers between devices, from_neighbours(): return (lax.ppermute(upper, axis, up), lax.ppermute(lower, axis, down))  26.5 us
    ppermute x5, starting transfers between devices, by_shifts(): lax.ppermute(part, axis, [(i, (i + shift) % size) for i in range(size)])  25 us
    all_to_all x3, starting transfers between devices, from_everyone(): return lax.all_to_all(copies, axis, split_axis=0, concat_axis=0, tiled=True)  24.4 us
    ppermute x4, starting transfers between devices, from_neighbours(): return (lax.ppermute(upper, axis, up), lax.ppermute(lower, axis, down))  22.9 us
    pallas_call x1, Pallas kernels, inverse_of(): pl.pallas_call(inverse_kernel, out_shape=jax.ShapeDtypeStruct(innovation....  22.1 us
    all_to_all x3, waiting for transfers between devices, from_everyone(): return lax.all_to_all(copies, axis, split_axis=0, concat_axis=0, tiled=True)  19.8 us
    dot_general x5, matrix products, contract(): return lax.dot_general(a, b, (dims, ((), ())), precision=finest_accuracy)  5.16 us
    ppermute x5, waiting for transfers between devices, by_shifts(): lax.ppermute(part, axis, [(i, (i + shift) % size) for i in range(size)])  3.43 us
  transfers between devices with their start and end apart: 12, of which 8 were waited for; matrix products, arithmetic and copies ran while one was open for 4% of the time, Pallas kernels for 13%

profile of v2, /device:TPU:16, one launch (start us, length us, event | category | flops | bytes accessed | tf_op | source)
XLA Modules:
  0.0 164.0 jit_solution(1253400404609238707)
XLA Ops:
  0.0 4.3 %collective-permute-start = (f32[256,512]{1,0:T(8,128)}, f32[256,512]{1,0:T(8,128)S(1)}, u32[]{:S(2)}, u32[]{:S(2)}) collective-permute-start(f32[256,512]{1,0:T(8,128)} %param.5), channel_id=1, source_target_pairs={{0,16},{16,32},{32,48},{48,64},{64,80},{80,96},{96,112},{112,128},... | collective-permute-start | bytes 1572872 | tf_op jit(solution)/shard_map/ppermute | solution.py:26
  4.3 5.4 %collective-permute-start.1 = (f32[256,512]{1,0:T(8,128)}, f32[256,512]{1,0:T(8,128)S(1)}, u32[]{:S(2)}, u32[]{:S(2)}) collective-permute-start(f32[256,512]{1,0:T(8,128)} %param.5), channel_id=1, source_target_pairs={{16,0},{32,16},{48,32},{64,48},{80,64},{96,80},{112,96},{128,112},... | collective-permute-start | bytes 1572872 | tf_op jit(solution)/shard_map/ppermute | solution.py:26
  9.8 0.8 slice_bitcast_fusion.3
  11.0 16.0 %collective-permute-done = f32[256,512]{1,0:T(8,128)S(1)} collective-permute-done((f32[256,512]{1,0:T(8,128)}, f32[256,512]{1,0:T(8,128)S(1)}, u32[]{:S(2)}, u32[]{:S(2)}) %collective-permute-start) | collective-permute-done | bytes 524320 | tf_op jit(solution)/shard_map/ppermute | solution.py:26
  27.0 4.1 %collective-permute-done.1 = f32[256,512]{1,0:T(8,128)S(1)} collective-permute-done((f32[256,512]{1,0:T(8,128)}, f32[256,512]{1,0:T(8,128)S(1)}, u32[]{:S(2)}, u32[]{:S(2)}) %collective-permute-start.1) | collective-permute-done | bytes 524320 | tf_op jit(solution)/shard_map/ppermute | solution.py:26
  31.1 1.2 pad_maximum_fusion
  33.8 0.7 fusion.7
  34.7 1.9 %collective-permute-start.2 = (f32[256,256]{1,0:T(8,128)S(1)}, f32[256,256]{1,0:T(8,128)S(1)}, u32[]{:S(2)}, u32[]{:S(2)}) collective-permute-start(f32[256,256]{1,0:T(8,128)S(1)} %get-tuple-element.49), channel_id=1, source_target_pairs={{0,1},{1,2},{2,3},{3,4},{4,5},{5,6},{6,7},{7,8},{8,9},{9,10},{10,1... | collective-permute-start | bytes 786440 | tf_op jit(solution)/shard_map/ppermute | solution.py:26
  36.7 11.3 %collective-permute-start.3 = (f32[256,256]{1,0:T(8,128)S(1)}, f32[256,256]{1,0:T(8,128)S(1)}, u32[]{:S(2)}, u32[]{:S(2)}) collective-permute-start(f32[256,256]{1,0:T(8,128)S(1)} %get-tuple-element.50), channel_id=1, source_target_pairs={{1,0},{2,1},{3,2},{4,3},{5,4},{6,5},{7,6},{8,7},{9,8},{10,9},{11,1... | collective-permute-start | bytes 786440 | tf_op jit(solution)/shard_map/ppermute | solution.py:26
  48.3 1.9 %collective-permute-done.2 = f32[256,256]{1,0:T(8,128)S(1)} collective-permute-done((f32[256,256]{1,0:T(8,128)S(1)}, f32[256,256]{1,0:T(8,128)S(1)}, u32[]{:S(2)}, u32[]{:S(2)}) %collective-permute-start.2) | collective-permute-done | bytes 262176 | tf_op jit(solution)/shard_map/ppermute | solution.py:26
  50.2 4.5 %collective-permute-done.3 = f32[256,256]{1,0:T(8,128)S(1)} collective-permute-done((f32[256,256]{1,0:T(8,128)S(1)}, f32[256,256]{1,0:T(8,128)S(1)}, u32[]{:S(2)}, u32[]{:S(2)}) %collective-permute-start.3) | collective-permute-done | bytes 262176 | tf_op jit(solution)/shard_map/ppermute | solution.py:26
  55.6 0.6 fusion.9
  57.3 0.9 fusion.11
  58.8 0.5 bitcast_dynamic-update-slice_fusion.7
  59.3 6.6 %collective-permute-start.4 = (f32[32,256]{1,0:T(8,128)S(1)}, f32[32,256]{1,0:T(8,128)S(1)}, u32[]{:S(2)}, u32[]{:S(2)}) collective-permute-start(f32[32,256]{1,0:T(8,128)S(1)} %get-tuple-element.72), channel_id=1, source_target_pairs={{0,1},{1,0},{2,3},{3,2},{4,5},{5,4},{6,7},{7,6},{8,9},{9,8},{10,11... | collective-permute-start | bytes 98312 | tf_op jit(solution)/shard_map/ppermute | solution.py:173
  66.6 0.7 broadcast_in_dim.79
  67.4 11.1 %all-to-all-start = ((f32[64,4,128]{2,1,0:T(4,128)}), f32[64,4,128]{2,1,0:T(4,128)S(1)}, u32[]{:S(2)}, u32[]{:S(2)}) async-start(f32[64,4,128]{2,1,0:T(4,128)} %broadcast_in_dim.79), calls=%async_computation | async-start | bytes 262144 | tf_op jit(solution)/shard_map/all_to_all | solution.py:19
  78.5 7.3 %collective-permute-start.5 = (f32[2,32,256]{2,1,0:T(8,128)S(1)}, f32[2,32,256]{2,1,0:T(8,128)S(1)}, u32[]{:S(2)}, u32[]{:S(2)}) collective-permute-start(f32[2,32,256]{2,1,0:T(8,128)S(1)} %bitcast_dynamic-update-slice_fusion.6), channel_id=1, source_target_pairs={{0,2},{2,0},{1,3},{3,1},{4,6},{6,4},{5,7},{7,5},{8,10},{10,8},{9,1... | collective-permute-start | bytes 196616 | tf_op jit(solution)/shard_map/ppermute | solution.py:173
  85.8 3.4 %collective-permute-done.5 = f32[2,32,256]{2,1,0:T(8,128)S(1)} collective-permute-done((f32[2,32,256]{2,1,0:T(8,128)S(1)}, f32[2,32,256]{2,1,0:T(8,128)S(1)}, u32[]{:S(2)}, u32[]{:S(2)}) %collective-permute-start.5) | collective-permute-done | bytes 65568 | tf_op jit(solution)/shard_map/ppermute | solution.py:173
  89.4 3.4 %collective-permute-start.6 = (f32[128,256]{1,0:T(8,128)S(1)}, f32[128,256]{1,0:T(8,128)S(1)}, u32[]{:S(2)}, u32[]{:S(2)}) collective-permute-start(f32[128,256]{1,0:T(8,128)S(1)} %bitcast.71), channel_id=1, source_target_pairs={{0,4},{4,8},{8,12},{12,0},{1,5},{5,9},{9,13},{13,1},{2,6},{6,10},{... | collective-permute-start | bytes 393224 | tf_op jit(solution)/shard_map/ppermute | solution.py:173
  92.8 3.6 %collective-permute-start.7 = (f32[128,256]{1,0:T(8,128)S(1)}, f32[128,256]{1,0:T(8,128)S(1)}, u32[]{:S(2)}, u32[]{:S(2)}) collective-permute-start(f32[128,256]{1,0:T(8,128)S(1)} %bitcast.72), channel_id=1, source_target_pairs={{0,8},{4,12},{8,0},{12,4},{1,9},{5,13},{9,1},{13,5},{2,10},{6,14},... | collective-permute-start | bytes 393224 | tf_op jit(solution)/shard_map/ppermute | solution.py:173
  96.4 4.1 %collective-permute-start.8 = (f32[128,256]{1,0:T(8,128)S(1)}, f32[128,256]{1,0:T(8,128)S(1)}, u32[]{:S(2)}, u32[]{:S(2)}) collective-permute-start(f32[128,256]{1,0:T(8,128)S(1)} %bitcast.73), channel_id=1, source_target_pairs={{0,12},{4,0},{8,4},{12,8},{1,13},{5,1},{9,5},{13,9},{2,14},{6,2},{... | collective-permute-start | bytes 393224 | tf_op jit(solution)/shard_map/ppermute | solution.py:173
  101.4 1.1 broadcast_in_dim.86
  102.5 3.6 %all-to-all-start.1 = ((f32[8,64,512]{2,1,0:T(8,128)}), f32[8,64,512]{2,1,0:T(8,128)S(1)}, u32[]{:S(2)}, u32[]{:S(2)}) async-start(f32[8,64,512]{2,1,0:T(8,128)} %broadcast_in_dim.86), calls=%async_computation.1 | async-start | bytes 2097152 | tf_op jit(solution)/shard_map/all_to_all | solution.py:19
  106.3 15.7 %all-to-all-done.1 = f32[8,64,512]{2,1,0:T(8,128)S(1)} async-done(((f32[8,64,512]{2,1,0:T(8,128)}), f32[8,64,512]{2,1,0:T(8,128)S(1)}, u32[]{:S(2)}, u32[]{:S(2)}) %all-to-all-start.1) | async-done | bytes 1048608 | tf_op jit(solution)/shard_map/all_to_all | solution.py:19
  121.9 1.1 copy.10
  123.0 1.1 broadcast_in_dim.93
  124.1 9.7 %all-to-all-start.2 = ((f32[32,16,512]{2,1,0:T(8,128)}), f32[32,16,512]{2,1,0:T(8,128)S(1)}, u32[]{:S(2)}, u32[]{:S(2)}) async-start(f32[32,16,512]{2,1,0:T(8,128)} %broadcast_in_dim.93), calls=%async_computation.2 | async-start | bytes 2097152 | tf_op jit(solution)/shard_map/all_to_all | solution.py:19
  133.9 22.1 %inverse_of.1 = f32[512,512]{1,0:T(8,128)} custom-call(f32[512,512]{1,0:T(8,128)} %bitcast.64, f32[1,512]{1,0:T(1,128)} %bitcast.75), custom_call_target="tpu_custom_call" | custom-call | tf_op jit(solution)/shard_map/inverse_of/pallas_call | solution.py:141
  156.0 2.2 %fusion.79 = f32[512,256]{1,0:T(8,128)S(1)} fusion(f32[512,512]{1,0:T(8,128)} %inverse_of.1, f32[512,256]{1,0:T(8,128)S(1)} %bitcast.70), kind=kOutput, calls=%fused_computation.149 | convolution fusion | flops 805306368 | bytes 2097152 | tf_op jit(solution)/shard_map/dot_general | solution.py:151
  158.2 4.0 %all-to-all-done.2 = f32[32,16,512]{2,1,0:T(8,128)S(1)} async-done(((f32[32,16,512]{2,1,0:T(8,128)}), f32[32,16,512]{2,1,0:T(8,128)S(1)}, u32[]{:S(2)}, u32[]{:S(2)}) %all-to-all-start.2) | async-done | bytes 1048608 | tf_op jit(solution)/shard_map/all_to_all | solution.py:19
  162.1 1.9 %convolution_subtract_fusion = f32[256,512]{1,0:T(8,128)} fusion(f32[512,256]{1,0:T(8,128)S(1)} %fusion.79, f32[512,512]{1,0:T(8,128)S(1)} %bitcast.63, f32[32,8,4,128]{3,2,1,0:T(4,128)S(1)} %bitcast.68, f32[256]{0:T(256)S(1)} %bitcast.78, s32[512]{0:T(512)S(1)} %iota_add_fusion, s32[256]{0:T(256)S(1)} %iota_add_fusion.1), kind=kOutput, calls=%fused_computation.5 | convolution fusion | flops 805830656 | bytes 2625536 | tf_op jit(solution)/shard_map/dot_general | solution.py:151
  (61 shorter events, 6.5 us)
Async XLA Ops:
  0.0 27.0 %collective-permute-start = (f32[256,512]{1,0:T(8,128)}, f32[256,512]{1,0:T(8,128)S(1)}, u32[]{:S(2)}, u32[]{:S(2)}) collective-permute-start(f32[256,512]{1,0:T(8,128)} %param.5), channel_id=1, source_target_pairs={{0,16},{16,32},{32,48},{48,64},{64,80},{80,96},{96,112},{112,128},... | collective-permute-start | bytes 1572872 | tf_op jit(solution)/shard_map/ppermute | solution.py:26
  4.3 26.9 %collective-permute-start.1 = (f32[256,512]{1,0:T(8,128)}, f32[256,512]{1,0:T(8,128)S(1)}, u32[]{:S(2)}, u32[]{:S(2)}) collective-permute-start(f32[256,512]{1,0:T(8,128)} %param.5), channel_id=1, source_target_pairs={{16,0},{32,16},{48,32},{64,48},{80,64},{96,80},{112,96},{128,112},... | collective-permute-start | bytes 1572872 | tf_op jit(solution)/shard_map/ppermute | solution.py:26
  34.5 13.6 %copy-start.1 = (s32[512]{0:T(512)S(1)}, s32[512]{0:T(512)}, u32[]{:S(2)}) copy-start(s32[512]{0:T(512)} %param.8) | copy-start | bytes 6148
  34.7 15.4 %collective-permute-start.2 = (f32[256,256]{1,0:T(8,128)S(1)}, f32[256,256]{1,0:T(8,128)S(1)}, u32[]{:S(2)}, u32[]{:S(2)}) collective-permute-start(f32[256,256]{1,0:T(8,128)S(1)} %get-tuple-element.49), channel_id=1, source_target_pairs={{0,1},{1,2},{2,3},{3,4},{4,5},{5,6},{6,7},{7,8},{8,9},{9,10},{10,1... | collective-permute-start | bytes 786440 | tf_op jit(solution)/shard_map/ppermute | solution.py:26
  36.7 18.0 %collective-permute-start.3 = (f32[256,256]{1,0:T(8,128)S(1)}, f32[256,256]{1,0:T(8,128)S(1)}, u32[]{:S(2)}, u32[]{:S(2)}) collective-permute-start(f32[256,256]{1,0:T(8,128)S(1)} %get-tuple-element.50), channel_id=1, source_target_pairs={{1,0},{2,1},{3,2},{4,3},{5,4},{6,5},{7,6},{8,7},{9,8},{10,9},{11,1... | collective-permute-start | bytes 786440 | tf_op jit(solution)/shard_map/ppermute | solution.py:26
  58.2 0.7 copy-start
  59.3 19.1 %collective-permute-start.4 = (f32[32,256]{1,0:T(8,128)S(1)}, f32[32,256]{1,0:T(8,128)S(1)}, u32[]{:S(2)}, u32[]{:S(2)}) collective-permute-start(f32[32,256]{1,0:T(8,128)S(1)} %get-tuple-element.72), channel_id=1, source_target_pairs={{0,1},{1,0},{2,3},{3,2},{4,5},{5,4},{6,7},{7,6},{8,9},{9,8},{10,11... | collective-permute-start | bytes 98312 | tf_op jit(solution)/shard_map/ppermute | solution.py:173
  67.4 22.0 %all-to-all-start = ((f32[64,4,128]{2,1,0:T(4,128)}), f32[64,4,128]{2,1,0:T(4,128)S(1)}, u32[]{:S(2)}, u32[]{:S(2)}) async-start(f32[64,4,128]{2,1,0:T(4,128)} %broadcast_in_dim.79), calls=%async_computation | async-start | bytes 262144 | tf_op jit(solution)/shard_map/all_to_all | solution.py:19
  78.5 10.7 %collective-permute-start.5 = (f32[2,32,256]{2,1,0:T(8,128)S(1)}, f32[2,32,256]{2,1,0:T(8,128)S(1)}, u32[]{:S(2)}, u32[]{:S(2)}) collective-permute-start(f32[2,32,256]{2,1,0:T(8,128)S(1)} %bitcast_dynamic-update-slice_fusion.6), channel_id=1, source_target_pairs={{0,2},{2,0},{1,3},{3,1},{4,6},{6,4},{5,7},{7,5},{8,10},{10,8},{9,1... | collective-permute-start | bytes 196616 | tf_op jit(solution)/shard_map/ppermute | solution.py:173
  89.4 16.8 %collective-permute-start.6 = (f32[128,256]{1,0:T(8,128)S(1)}, f32[128,256]{1,0:T(8,128)S(1)}, u32[]{:S(2)}, u32[]{:S(2)}) collective-permute-start(f32[128,256]{1,0:T(8,128)S(1)} %bitcast.71), channel_id=1, source_target_pairs={{0,4},{4,8},{8,12},{12,0},{1,5},{5,9},{9,13},{13,1},{2,6},{6,10},{... | collective-permute-start | bytes 393224 | tf_op jit(solution)/shard_map/ppermute | solution.py:173
  92.8 13.4 %collective-permute-start.7 = (f32[128,256]{1,0:T(8,128)S(1)}, f32[128,256]{1,0:T(8,128)S(1)}, u32[]{:S(2)}, u32[]{:S(2)}) collective-permute-start(f32[128,256]{1,0:T(8,128)S(1)} %bitcast.72), channel_id=1, source_target_pairs={{0,8},{4,12},{8,0},{12,4},{1,9},{5,13},{9,1},{13,5},{2,10},{6,14},... | collective-permute-start | bytes 393224 | tf_op jit(solution)/shard_map/ppermute | solution.py:173
  96.4 9.8 %collective-permute-start.8 = (f32[128,256]{1,0:T(8,128)S(1)}, f32[128,256]{1,0:T(8,128)S(1)}, u32[]{:S(2)}, u32[]{:S(2)}) collective-permute-start(f32[128,256]{1,0:T(8,128)S(1)} %bitcast.73), channel_id=1, source_target_pairs={{0,12},{4,0},{8,4},{12,8},{1,13},{5,1},{9,5},{13,9},{2,14},{6,2},{... | collective-permute-start | bytes 393224 | tf_op jit(solution)/shard_map/ppermute | solution.py:173
  102.5 19.4 %all-to-all-start.1 = ((f32[8,64,512]{2,1,0:T(8,128)}), f32[8,64,512]{2,1,0:T(8,128)S(1)}, u32[]{:S(2)}, u32[]{:S(2)}) async-start(f32[8,64,512]{2,1,0:T(8,128)} %broadcast_in_dim.86), calls=%async_computation.1 | async-start | bytes 2097152 | tf_op jit(solution)/shard_map/all_to_all | solution.py:19
  124.1 38.0 %all-to-all-start.2 = ((f32[32,16,512]{2,1,0:T(8,128)}), f32[32,16,512]{2,1,0:T(8,128)S(1)}, u32[]{:S(2)}, u32[]{:S(2)}) async-start(f32[32,16,512]{2,1,0:T(8,128)} %broadcast_in_dim.93), calls=%async_computation.2 | async-start | bytes 2097152 | tf_op jit(solution)/shard_map/all_to_all | solution.py:19

commit v3 on v2

--- a/solution.py
+++ b/solution.py
@@ -9,6 +9,9 @@
 CYCLES = 2
 TILE = 128
 GROUP = 8
+STRIP = 32
+CORES = 2
+HALVES = 2
 
 
 finest_accuracy = lax.Precision.HIGHEST
@@ -103,48 +106,94 @@
     return jnp.dot(a, b, precision=finest_accuracy, preferred_element_type=jnp.float32)
 
 
-def inverse_kernel(innovation_ref, noise_ref, out_ref):
-    size = innovation_ref.shape[0]
+def solve_kernel(slabs_ref, noise_ref, out_ref, work):
+    size = noise_ref.shape[1]
     lane = lax.broadcasted_iota(jnp.int32, (GROUP, TILE), 1)
     sub = lax.broadcasted_iota(jnp.int32, (GROUP, TILE), 0)
-    square = innovation_ref[...]
+    slabs, share = slabs_ref.shape[0], slabs_ref.shape[1] // HALVES
+    for n in range(slabs):
+        for half in range(HALVES):
+            place = (n // CORES * HALVES + half) * CORES + n % CORES
+            work[place * share : (place + 1) * share, :] = slabs_ref[
+                n, half * share : (half + 1) * share, :
+            ]
+    square = work[:, :size]
     square = 0.5 * (square + square.T)
     diagonal = lax.broadcasted_iota(jnp.int32, (size, size), 0) == lax.broadcasted_iota(
         jnp.int32, (size, size), 1
     )
-    out_ref[...] = jnp.where(diagonal, square + noise_ref[...], square)
+    work[:, :size] = jnp.where(diagonal, square + noise_ref[...], square)
     tiles = size // TILE
-    spans = [slice(t * TILE, (t + 1) * TILE) for t in range(tiles)]
     for t in range(tiles):
-        here = spans[t]
-        rows = [
-            out_ref[t * TILE + GROUP * i : t * TILE + GROUP * (i + 1), here]
-            for i in range(TILE // GROUP)
-        ]
+        lo, hi = t * TILE, (t + 1) * TILE
+        rows = [work[lo + GROUP * i : lo + GROUP * (i + 1), lo:hi] for i in range(TILE // GROUP)]
         inverse = jnp.concatenate(inverse_tile(rows, lane, sub), axis=0)
-        for j in range(tiles):
-            if j != t:
-                out_ref[here, spans[j]] = exact_dot(inverse, out_ref[here, spans[j]])
+        solved = exact_dot(inverse, work[lo:hi, hi:])
         for i in range(tiles):
             if i != t:
-                column = out_ref[spans[i], here]
-                for j in range(tiles):
-                    if j != t:
-                        out_ref[spans[i], spans[j]] = out_ref[spans[i], spans[j]] - exact_dot(
-                            column, out_ref[here, spans[j]]
-                        )
-                out_ref[spans[i], here] = -exact_dot(column, inverse)
-        out_ref[here, here] = inverse
-
-
-def inverse_of(innovation, noise):
+                span = slice(i * TILE, (i + 1) * TILE)
+                work[span, hi:] = work[span, hi:] - exact_dot(work[span, lo:hi], solved)
+        work[lo:hi, hi:] = solved
+    out_ref[...] = work[:, size:]
+
+
+def solve_gain(slabs, noise):
+    size, wide = noise.shape[0], slabs.shape[2]
     return pl.pallas_call(
-        inverse_kernel,
-        out_shape=jax.ShapeDtypeStruct(innovation.shape, jnp.float32),
+        solve_kernel,
+        out_shape=jax.ShapeDtypeStruct((size, wide - size), jnp.float32),
         in_specs=[pl.BlockSpec(memory_space=pltpu.VMEM)] * 2,
         out_specs=pl.BlockSpec(memory_space=pltpu.VMEM),
-        name="inverse_of",
-    )(innovation, noise[None, :])
+        scratch_shapes=[pltpu.VMEM((size, wide), jnp.float32)],
+        name="solve_gain",
+    )(slabs, noise[None, :])
+
+
+def columns_kernel(*refs):
+    fields, winds, (noise_ref, shift_ref, out_ref) = refs[:4], refs[4:8], refs[8:]
+    height = out_ref.shape[0]
+    for start in range(0, height, STRIP):
+        strip = slice(start, start + STRIP)
+        tiles = [
+            ref[strip, k * NC : (k + 1) * NC]
+            for ref in fields
+            for k in range(ref.shape[1] // NC)
+        ]
+        for cycle in range(CYCLES):
+            east, north = winds[2 * cycle][...], winds[2 * cycle + 1][...]
+            behind, centre, ahead = stencil_weights(east)
+            tiles = [
+                behind[i : i + 1] * pltpu.roll(tile, 1, 1)
+                + centre[i : i + 1] * tile
+                + ahead[i : i + 1] * pltpu.roll(tile, NC - 1, 1)
+                for i, tile in enumerate(tiles)
+            ]
+            behind, centre, ahead = stencil_weights(north)
+            tiles = [
+                behind[i : i + 1] * tiles[i]
+                + centre[i : i + 1] * tiles[i + 1]
+                + ahead[i : i + 1] * tiles[i + 2]
+                for i in range(len(tiles) - 2)
+            ]
+        row = lax.broadcasted_iota(jnp.int32, (STRIP, NC), 0) + (shift_ref[0] + start)
+        column = lax.broadcasted_iota(jnp.int32, (STRIP, NC), 1)
+        for i, tile in enumerate(tiles):
+            here = slice(i * NC, (i + 1) * NC)
+            out_ref[strip, here] = tile + jnp.where(
+                row == column + i * NC, noise_ref[:, here], 0.0
+            )
+
+
+def columns_forecast(fields, winds, noise, shift):
+    height = fields[0].shape[0]
+    return pl.pallas_call(
+        columns_kernel,
+        out_shape=jax.ShapeDtypeStruct((height, noise.shape[1]), jnp.float32),
+        in_specs=[pl.BlockSpec(memory_space=pltpu.VMEM)] * 9
+        + [pl.BlockSpec(memory_space=pltpu.SMEM)],
+        out_specs=pl.BlockSpec(memory_space=pltpu.VMEM),
+        name="columns_forecast",
+    )(*fields, *winds, noise, shift)
 
 
 def contract(a, b, dims):
@@ -156,13 +205,6 @@
     field = sweep_local(field, wind_rows(courants, cycle, 0, first, length)[:, :, None], 1)
     north = wind_rows(courants, cycle, 1, first + 1, length - 2)[:, :, None]
     return sweep_padded(field, north, 0)
-
-
-def step_columns(field, courants, cycle, first):
-    length = field.shape[1]
-    field = sweep_local(field, wind_rows(courants, cycle, 0, first, length)[None], 2)
-    north = wind_rows(courants, cycle, 1, first + 1, length - 2)[None]
-    return sweep_padded(field, north, 1)
 
 
 def by_shifts(part, axis):
@@ -182,23 +224,32 @@
     row_first, column_first = row_index * band_rows, column_index * band_columns
     edge = CYCLES * NC
 
-    before, after = from_neighbours(covariance[:edge], covariance[height - edge :], ROW)
-    field = jnp.concatenate([before, covariance, after], axis=0).reshape(-1, NC, width)
+    halves = []
+    for part in (covariance[:, width - edge :], covariance[:, :edge]):
+        before, after = from_neighbours(part[:edge], part[height - edge :], ROW)
+        if halves:
+            before, after, _ = lax.optimization_barrier((before, after, halves[0]))
+        field = jnp.concatenate([before, part, after], axis=0).reshape(-1, NC, edge)
+        for cycle in range(CYCLES):
+            field = step_rows(field, courants, cycle, row_first - CYCLES + cycle)
+        halves.append(field.reshape(height, edge))
+    upper, lower = halves
+    before, after = from_neighbours(lower, upper, COL)
+    winds = []
     for cycle in range(CYCLES):
-        field = step_rows(field, courants, cycle, row_first - CYCLES + cycle)
-    half_way = field.reshape(height, width)
-
-    before, after = from_neighbours(half_way[:, :edge], half_way[:, width - edge :], COL)
-    field = jnp.concatenate([before, half_way, after], axis=1).reshape(height, -1, NC)
-    for cycle in range(CYCLES):
-        field = step_columns(field, courants, cycle, column_first - CYCLES + cycle)
-    forecast = field.reshape(height, width)
-
+        first, length = column_first - CYCLES + cycle, band_columns + 2 * (CYCLES - cycle)
+        winds.append(wind_rows(courants, cycle, 0, first, length))
+        winds.append(wind_rows(courants, cycle, 1, first + 1, length - 2))
+    noise_here = process_noise_spread.reshape(1, height)
+    offset = row_first - column_first
+    noise_columns = jnp.concatenate(
+        [jnp.where(offset == k, noise_here, 0.0) for k in range(0, band_columns, band_rows)], axis=1
+    )
+    forecast = columns_forecast(
+        (before, lower, upper, after), winds, noise_columns, jnp.reshape(offset * NC, (1,))
+    )
     row_ids = row_index * height + jnp.arange(height, dtype=jnp.int32)
     column_ids = column_index * width + jnp.arange(width, dtype=jnp.int32)
-    forecast = forecast + jnp.where(
-        row_ids[:, None] == column_ids[None, :], process_noise_spread.reshape(height, 1), 0.0
-    )
 
     sensors = sensor_targets.shape[0]
     row_share = sensors // lax.axis_size(ROW)
@@ -215,18 +266,15 @@
 
     high = lax.axis_size("zh")
     block = from_everyone(block.reshape(-1, NC), ("y", "zl", "zh"))
-    gain = by_shifts(by_shifts(gain, "core"), "zh").reshape(-1, height)
+    gain = by_shifts(gain, "zh").reshape(-1, height)
     block, gain, obs = lax.optimization_barrier((block, gain, obs))
     block = block.reshape(-1, high, row_share, column_share)
     slab = block.transpose(1, 3, 0, 2).reshape(high * column_share, sensors)
-    slabs = from_everyone(slab, ("x", "core"))
-    flat = (lax.axis_size("x"), lax.axis_size("core"), high, column_share, sensors)
-    innovation = slabs.reshape(flat).transpose(0, 2, 1, 3, 4).reshape(sensors, sensors)
-
-    gain = by_shifts(gain, "x").reshape(sensors, height)
-    innovation, gain, obs = lax.optimization_barrier((innovation, gain, obs))
+    slabs = from_everyone(jnp.concatenate([slab, gain], axis=1), ("x", "core"))
+    slabs, obs = lax.optimization_barrier((slabs, obs))
+
     obs_rows = from_everyone(obs, ROW).reshape(sensors, width)
-    solved = contract(inverse_of(innovation, noise_variance), gain, ((1,), (0,)))
+    solved = solve_gain(slabs, noise_variance)
     return forecast - contract(solved, obs_rows, ((0,), (0,)))
 
 
@@ -236,7 +284,7 @@
 
 def physical(mesh):
     rows, columns = mesh.devices.shape
-    zl, zh, core = 4, 2, 2
+    zl, zh, core = 4, HALVES, CORES
     shape = (rows // zl, zl, columns // (zh * core), zh, core)
     return jax.sharding.Mesh(mesh.devices.reshape(shape), ROW + COL)
 

time: 165 us -> 152 us (0.921)
  blocking collectives: 0 us -> 26.7 us
  waiting for transfers between devices: 49.8 us -> 27.7 us
  starting transfers between devices: 72.3 us -> 54.1 us
  Pallas kernels: 22.1 us -> 25.2 us
  local copies, waits for them, and re-layouts: 8.71 us -> 6.28 us
    all_to_all x0 -> x1, blocking collectives: none -> 26.7 us  [from_everyone(): return lax.all_to_all(copies, axis, split_axis=0, concat_axis=0, tiled=True)]
    ppermute x5 -> x1, starting transfers between devices: 25 us -> 4.73 us  [by_shifts(): lax.ppermute(part, axis, [(i, (i + shift) % size) for i in range(size)])]
    ppermute x4 -> x6, waiting for transfers between devices: 26.5 us -> 10.5 us  [from_neighbours(): return (lax.ppermute(upper, axis, up), lax.ppermute(lower, axis, down))]
    ppermute x4 -> x6, starting transfers between devices: 22.9 us -> 30.2 us  [from_neighbours(): return (lax.ppermute(upper, axis, up), lax.ppermute(lower, axis, down))]
    all_to_all x3 -> x2, starting transfers between devices: 24.4 us -> 19.2 us  [from_everyone(): return lax.all_to_all(copies, axis, split_axis=0, concat_axis=0, tiled=True)]
    ppermute x5 -> x1, waiting for transfers between devices: 3.43 us -> 0.01 us  [by_shifts(): lax.ppermute(part, axis, [(i, (i + shift) % size) for i in range(size)])]
    pallas_call x1 -> x2, Pallas kernels: 22.1 us -> 25.2 us  [the longest x1 22 us: solve_gain(): pl.pallas_call(solve_kernel, out_shape=jax.ShapeDtypeStruct((size, wide -...]
    all_to_all x3 -> x2, waiting for transfers between devices: 19.8 us -> 17.2 us  [from_everyone(): return lax.all_to_all(copies, axis, split_axis=0, concat_axis=0, tiled=True)]
  transfers between devices with their start and end apart: 12 -> 9, of which waited for: 8 -> 6; matrix products, arithmetic and copies ran while one was open for 4% -> 6% of each run, Pallas kernels for 13% -> 14%
where the time goes in v3:
time: 152 us
  starting transfers between devices  54.1 us (36%)
  waiting for transfers between devices  27.7 us (18%)
  blocking collectives  26.7 us (18%)
  Pallas kernels  25.2 us (17%)
  local copies, waits for them, and re-layouts  6.28 us (4%)
  matrix products  5.85 us (4%)
  other arithmetic  5.25 us (3%)
    ppermute x6, starting transfers between devices, from_neighbours(): return (lax.ppermute(upper, axis, up), lax.ppermute(lower, axis, down))  30.2 us
    all_to_all x1, blocking collectives, from_everyone(): return lax.all_to_all(copies, axis, split_axis=0, concat_axis=0, tiled=True)  26.7 us
    pallas_call x1, Pallas kernels, solve_gain(): pl.pallas_call(solve_kernel, out_shape=jax.ShapeDtypeStruct((size, wide -...  22 us
    all_to_all x2, starting transfers between devices, from_everyone(): return lax.all_to_all(copies, axis, split_axis=0, concat_axis=0, tiled=True)  19.2 us
    all_to_all x2, waiting for transfers between devices, from_everyone(): return lax.all_to_all(copies, axis, split_axis=0, concat_axis=0, tiled=True)  17.2 us
    ppermute x6, waiting for transfers between devices, from_neighbours(): return (lax.ppermute(upper, axis, up), lax.ppermute(lower, axis, down))  10.5 us
    dot_general x4, matrix products, contract(): return lax.dot_general(a, b, (dims, ((), ())), precision=finest_accuracy)  5.85 us
    ppermute x1, starting transfers between devices, by_shifts(): lax.ppermute(part, axis, [(i, (i + shift) % size) for i in range(size)])  4.73 us
  transfers between devices with their start and end apart: 9, of which 6 were waited for; matrix products, arithmetic and copies ran while one was open for 6% of the time, Pallas kernels for 14%

profile of v3, /device:TPU:16, one launch (start us, length us, event | category | flops | bytes accessed | tf_op | source)
XLA Modules:
  0.0 151.7 jit_solution(6170249278534715422)
XLA Ops:
  0.0 1.1 fusion.54
  1.1 7.8 %collective-permute-start.1 = (f32[256,256]{1,0:T(8,128)S(1)}, f32[256,256]{1,0:T(8,128)S(1)}, u32[]{:S(2)}, u32[]{:S(2)}) collective-permute-start(f32[256,256]{1,0:T(8,128)S(1)} %get-tuple-element.40), channel_id=1, source_target_pairs={{16,0},{32,16},{48,32},{64,48},{80,64},{96,80},{112,96},{128,112},... | collective-permute-start | bytes 786440 | tf_op jit(solution)/shard_map/ppermute | solution.py:29
  8.9 1.9 %collective-permute-start = (f32[256,256]{1,0:T(8,128)S(1)}, f32[256,256]{1,0:T(8,128)S(1)}, u32[]{:S(2)}, u32[]{:S(2)}) collective-permute-start(f32[256,256]{1,0:T(8,128)S(1)} %get-tuple-element.40), channel_id=1, source_target_pairs={{0,16},{16,32},{32,48},{48,64},{64,80},{80,96},{96,112},{112,128},... | collective-permute-start | bytes 786440 | tf_op jit(solution)/shard_map/ppermute | solution.py:29
  10.8 1.9 %collective-permute-start.3 = (f32[256,256]{1,0:T(8,128)S(1)}, f32[256,256]{1,0:T(8,128)S(1)}, u32[]{:S(2)}, u32[]{:S(2)}) collective-permute-start(f32[256,256]{1,0:T(8,128)S(1)} %get-tuple-element.39), channel_id=1, source_target_pairs={{0,16},{16,32},{32,48},{48,64},{64,80},{80,96},{96,112},{112,128},... | collective-permute-start | bytes 786440 | tf_op jit(solution)/shard_map/ppermute | solution.py:29
  12.7 6.6 %collective-permute-start.4 = (f32[256,256]{1,0:T(8,128)S(1)}, f32[256,256]{1,0:T(8,128)S(1)}, u32[]{:S(2)}, u32[]{:S(2)}) collective-permute-start(f32[256,256]{1,0:T(8,128)S(1)} %get-tuple-element.39), channel_id=1, source_target_pairs={{16,0},{32,16},{48,32},{64,48},{80,64},{96,80},{112,96},{128,112},... | collective-permute-start | bytes 786440 | tf_op jit(solution)/shard_map/ppermute | solution.py:29
  19.4 0.8 slice_bitcast_fusion.3
  20.4 0.6 fusion.34.refs_7_
  21.0 0.6 pad_maximum_fusion.3.refs_8_
  21.6 5.1 %collective-permute-done = f32[256,256]{1,0:T(8,128)S(1)} collective-permute-done((f32[256,256]{1,0:T(8,128)S(1)}, f32[256,256]{1,0:T(8,128)S(1)}, u32[]{:S(2)}, u32[]{:S(2)}) %collective-permute-start) | collective-permute-done | bytes 262176 | tf_op jit(solution)/shard_map/ppermute | solution.py:29
  27.0 0.4 fusion.1
  27.7 0.5 fusion.9
  28.4 1.9 %collective-permute-start.2 = (f32[256,256]{1,0:T(8,128)S(1)}, f32[256,256]{1,0:T(8,128)S(1)}, u32[]{:S(2)}, u32[]{:S(2)}) collective-permute-start(f32[256,256]{1,0:T(8,128)S(1)} %bitcast.38), channel_id=1, source_target_pairs={{0,1},{1,2},{2,3},{3,4},{4,5},{5,6},{6,7},{7,8},{8,9},{9,10},{10,1... | collective-permute-start | bytes 786440 | tf_op jit(solution)/shard_map/ppermute | solution.py:29
  30.3 1.9 %collective-permute-done.3 = f32[256,256]{1,0:T(8,128)S(1)} collective-permute-done((f32[256,256]{1,0:T(8,128)S(1)}, f32[256,256]{1,0:T(8,128)S(1)}, u32[]{:S(2)}, u32[]{:S(2)}) %collective-permute-start.3) | collective-permute-done | bytes 262176 | tf_op jit(solution)/shard_map/ppermute | solution.py:29
  33.5 0.5 fusion.11
  34.1 10.0 %collective-permute-start.5 = (f32[256,256]{1,0:T(8,128)S(1)}, f32[256,256]{1,0:T(8,128)S(1)}, u32[]{:S(2)}, u32[]{:S(2)}) collective-permute-start(f32[256,256]{1,0:T(8,128)S(1)} %bitcast.40), channel_id=1, source_target_pairs={{1,0},{2,1},{3,2},{4,3},{5,4},{6,5},{7,6},{8,7},{9,8},{10,9},{11,1... | collective-permute-start | bytes 786440 | tf_op jit(solution)/shard_map/ppermute | solution.py:29
  44.4 0.6 fusion.32.refs_4_
  45.0 0.6 fusion.30
  45.6 3.3 %collective-permute-done.5.refs_3_ = f32[256,256]{1,0:T(8,128)S(1)} collective-permute-done((f32[256,256]{1,0:T(8,128)S(1)}, f32[256,256]{1,0:T(8,128)S(1)}, u32[]{:S(2)}, u32[]{:S(2)}) %collective-permute-start.5) | collective-permute-done | bytes 262176 | tf_op jit(solution)/shard_map/ppermute | solution.py:29
  48.9 0.7 copy-done.4
  49.6 3.2 %columns_forecast.1 = f32[256,512]{1,0:T(8,128)} custom-call(f32[256,256]{1,0:T(8,128)} %copy-done.3, f32[256,256]{1,0:T(8,128)} %bitcast.41, f32[256,256]{1,0:T(8,128)} %bitcast.39, f32[256,256]{1,0:T(8,128)} %copy-done.4, f32[8,128]{1,0:T(8,128)} %fusion.32.refs_4_, f32[6,128]{1,0:T(8,128)} %get-tuple-element.61.refs_5_, ...), custom_call_target="tpu_custom_call" | custom-call | tf_op jit(solution)/shard_map/columns_forecast/pallas_call | solution.py:189
  52.9 1.4 bitcast_dynamic-update-slice_fusion.1
  54.3 4.7 %collective-permute-start.6 = (f32[32,256]{1,0:T(8,128)S(1)}, f32[32,256]{1,0:T(8,128)S(1)}, u32[]{:S(2)}, u32[]{:S(2)}) collective-permute-start(f32[32,256]{1,0:T(8,128)S(1)} %get-tuple-element.60), channel_id=1, source_target_pairs={{0,2},{2,0},{1,3},{3,1},{4,6},{6,4},{5,7},{7,5},{8,10},{10,8},{9,1... | collective-permute-start | bytes 98312 | tf_op jit(solution)/shard_map/ppermute | solution.py:215
  59.0 1.3 fusion.24
  60.7 0.7 broadcast_in_dim.40
  61.4 12.6 %all-to-all-start = ((f32[64,4,128]{2,1,0:T(4,128)}), f32[64,4,128]{2,1,0:T(4,128)S(1)}, u32[]{:S(2)}, u32[]{:S(2)}) async-start(f32[64,4,128]{2,1,0:T(4,128)} %broadcast_in_dim.40), calls=%async_computation | async-start | bytes 262144 | tf_op jit(solution)/shard_map/all_to_all | solution.py:22
  74.0 10.6 %all-to-all-done = f32[64,4,128]{2,1,0:T(4,128)S(1)} async-done(((f32[64,4,128]{2,1,0:T(4,128)}), f32[64,4,128]{2,1,0:T(4,128)S(1)}, u32[]{:S(2)}, u32[]{:S(2)}) %all-to-all-start) | async-done | bytes 131104 | tf_op jit(solution)/shard_map/all_to_all | solution.py:22
  85.8 26.7 %all_to_all.15.slabs_ref = f32[8,64,768]{2,1,0:T(8,128)} all-to-all(f32[8,64,768]{2,1,0:T(8,128)S(1)} %broadcast_in_dim.44), channel_id=1, replica_groups=mesh['y'=8,'zl'=4,'x'=4,'zh'=2,'core'=2] {'x','core'}, dimensions={0} | all-to-all | bytes 3145728 | tf_op jit(solution)/shard_map/all_to_all | solution.py:22
  112.5 1.1 broadcast_in_dim.46
  113.7 6.6 %all-to-all-start.2 = ((f32[32,16,512]{2,1,0:T(8,128)}), f32[32,16,512]{2,1,0:T(8,128)S(1)}, u32[]{:S(2)}, u32[]{:S(2)}) async-start(f32[32,16,512]{2,1,0:T(8,128)} %broadcast_in_dim.46), calls=%async_computation.2 | async-start | bytes 2097152 | tf_op jit(solution)/shard_map/all_to_all | solution.py:22
  120.3 22.0 %solve_gain.1 = f32[512,256]{1,0:T(8,128)} custom-call(f32[8,64,768]{2,1,0:T(8,128)} %all_to_all.15.slabs_ref, f32[1,512]{1,0:T(1,128)} %bitcast.45), custom_call_target="tpu_custom_call" | custom-call | tf_op jit(solution)/shard_map/solve_gain/pallas_call | solution.py:142
  142.3 6.5 %all-to-all-done.2 = f32[32,16,512]{2,1,0:T(8,128)S(1)} async-done(((f32[32,16,512]{2,1,0:T(8,128)}), f32[32,16,512]{2,1,0:T(8,128)S(1)}, u32[]{:S(2)}, u32[]{:S(2)}) %all-to-all-start.2) | async-done | bytes 1048608 | tf_op jit(solution)/shard_map/all_to_all | solution.py:22
  148.8 2.9 %convolution_subtract_fusion = f32[256,512]{1,0:T(8,128)} fusion(f32[256,512]{1,0:T(8,128)S(1)} %copy-done, f32[512,256]{1,0:T(8,128)} %solve_gain.1, f32[512,512]{1,0:T(8,128)S(1)} %bitcast.36), kind=kOutput, calls=%fused_computation | convolution fusion | flops 805437440 | bytes 2621440 | tf_op jit(solution)/shard_map/dot_general | solution.py:200
  (56 shorter events, 3.8 us)
Async XLA Ops:
  0.0 21.0 %copy-start.5 = (f32[2,128]{1,0:T(2,128)S(1)}, f32[2,128]{1,0:T(2,128)}, u32[]{:S(2)}) copy-start(f32[2,128]{1,0:T(2,128)} %param.7) | copy-start | bytes 3076
  1.1 20.6 %collective-permute-start.1 = (f32[256,256]{1,0:T(8,128)S(1)}, f32[256,256]{1,0:T(8,128)S(1)}, u32[]{:S(2)}, u32[]{:S(2)}) collective-permute-start(f32[256,256]{1,0:T(8,128)S(1)} %get-tuple-element.40), channel_id=1, source_target_pairs={{16,0},{32,16},{48,32},{64,48},{80,64},{96,80},{112,96},{128,112},... | collective-permute-start | bytes 786440 | tf_op jit(solution)/shard_map/ppermute | solution.py:29
  8.9 17.9 %collective-permute-start = (f32[256,256]{1,0:T(8,128)S(1)}, f32[256,256]{1,0:T(8,128)S(1)}, u32[]{:S(2)}, u32[]{:S(2)}) collective-permute-start(f32[256,256]{1,0:T(8,128)S(1)} %get-tuple-element.40), channel_id=1, source_target_pairs={{0,16},{16,32},{32,48},{48,64},{64,80},{80,96},{96,112},{112,128},... | collective-permute-start | bytes 786440 | tf_op jit(solution)/shard_map/ppermute | solution.py:29
  10.8 21.5 %collective-permute-start.3 = (f32[256,256]{1,0:T(8,128)S(1)}, f32[256,256]{1,0:T(8,128)S(1)}, u32[]{:S(2)}, u32[]{:S(2)}) collective-permute-start(f32[256,256]{1,0:T(8,128)S(1)} %get-tuple-element.39), channel_id=1, source_target_pairs={{0,16},{16,32},{32,48},{48,64},{64,80},{80,96},{96,112},{112,128},... | collective-permute-start | bytes 786440 | tf_op jit(solution)/shard_map/ppermute | solution.py:29
  12.7 19.7 %collective-permute-start.4 = (f32[256,256]{1,0:T(8,128)S(1)}, f32[256,256]{1,0:T(8,128)S(1)}, u32[]{:S(2)}, u32[]{:S(2)}) collective-permute-start(f32[256,256]{1,0:T(8,128)S(1)} %get-tuple-element.39), channel_id=1, source_target_pairs={{16,0},{32,16},{48,32},{64,48},{80,64},{96,80},{112,96},{128,112},... | collective-permute-start | bytes 786440 | tf_op jit(solution)/shard_map/ppermute | solution.py:29
  28.4 4.3 %copy-start.1 = (f32[2,128,256]{2,1,0:T(8,128)}, f32[2,128,256]{2,1,0:T(8,128)S(1)}, u32[]{:S(2)}) copy-start(f32[2,128,256]{2,1,0:T(8,128)S(1)} %fusion.14) | copy-start | bytes 786436
  28.4 17.2 %collective-permute-start.2 = (f32[256,256]{1,0:T(8,128)S(1)}, f32[256,256]{1,0:T(8,128)S(1)}, u32[]{:S(2)}, u32[]{:S(2)}) collective-permute-start(f32[256,256]{1,0:T(8,128)S(1)} %bitcast.38), channel_id=1, source_target_pairs={{0,1},{1,2},{2,3},{3,4},{4,5},{5,6},{6,7},{7,8},{8,9},{9,10},{10,1... | collective-permute-start | bytes 786440 | tf_op jit(solution)/shard_map/ppermute | solution.py:29
  33.5 10.8 %copy-start.6 = (s32[512]{0:T(512)S(1)}, s32[512]{0:T(512)}, u32[]{:S(2)}) copy-start(s32[512]{0:T(512)} %param.8) | copy-start | bytes 6148
  34.1 14.8 %copy-start.2 = (f32[2,128,256]{2,1,0:T(8,128)}, f32[2,128,256]{2,1,0:T(8,128)S(1)}, u32[]{:S(2)}) copy-start(f32[2,128,256]{2,1,0:T(8,128)S(1)} %fusion.12) | copy-start | bytes 786436
  34.1 14.8 %collective-permute-start.5 = (f32[256,256]{1,0:T(8,128)S(1)}, f32[256,256]{1,0:T(8,128)S(1)}, u32[]{:S(2)}, u32[]{:S(2)}) collective-permute-start(f32[256,256]{1,0:T(8,128)S(1)} %bitcast.40), channel_id=1, source_target_pairs={{1,0},{2,1},{3,2},{4,3},{5,4},{6,5},{7,6},{8,7},{9,8},{10,9},{11,1... | collective-permute-start | bytes 786440 | tf_op jit(solution)/shard_map/ppermute | solution.py:29
  45.6 3.3 %copy-start.3 = (f32[256,256]{1,0:T(8,128)}, f32[256,256]{1,0:T(8,128)S(1)}, u32[]{:S(2)}) copy-start(f32[256,256]{1,0:T(8,128)S(1)} %collective-permute-done.2.refs_0_) | copy-start | bytes 786436
  48.9 0.7 copy-start.4
  54.3 19.7 %collective-permute-start.6 = (f32[32,256]{1,0:T(8,128)S(1)}, f32[32,256]{1,0:T(8,128)S(1)}, u32[]{:S(2)}, u32[]{:S(2)}) collective-permute-start(f32[32,256]{1,0:T(8,128)S(1)} %get-tuple-element.60), channel_id=1, source_target_pairs={{0,2},{2,0},{1,3},{3,1},{4,6},{6,4},{5,7},{7,5},{8,10},{10,8},{9,1... | collective-permute-start | bytes 98312 | tf_op jit(solution)/shard_map/ppermute | solution.py:215
  61.4 23.3 %all-to-all-start = ((f32[64,4,128]{2,1,0:T(4,128)}), f32[64,4,128]{2,1,0:T(4,128)S(1)}, u32[]{:S(2)}, u32[]{:S(2)}) async-start(f32[64,4,128]{2,1,0:T(4,128)} %broadcast_in_dim.40), calls=%async_computation | async-start | bytes 262144 | tf_op jit(solution)/shard_map/all_to_all | solution.py:22
  113.7 35.1 %all-to-all-start.2 = ((f32[32,16,512]{2,1,0:T(8,128)}), f32[32,16,512]{2,1,0:T(8,128)S(1)}, u32[]{:S(2)}, u32[]{:S(2)}) async-start(f32[32,16,512]{2,1,0:T(8,128)} %broadcast_in_dim.46), calls=%async_computation.2 | async-start | bytes 2097152 | tf_op jit(solution)/shard_map/all_to_all | solution.py:22
  120.3 28.5 %copy-start = (f32[256,512]{1,0:T(8,128)S(1)}, f32[256,512]{1,0:T(8,128)}, u32[]{:S(2)}) copy-start(f32[256,512]{1,0:T(8,128)} %columns_forecast.1) | copy-start | bytes 1572868

commit v4 on v3

--- a/solution.py
+++ b/solution.py
@@ -9,7 +9,7 @@
 CYCLES = 2
 TILE = 128
 GROUP = 8
-STRIP = 32
+STRIP = 64
 CORES = 2
 HALVES = 2
 
@@ -124,16 +124,26 @@
     )
     work[:, :size] = jnp.where(diagonal, square + noise_ref[...], square)
     tiles = size // TILE
-    for t in range(tiles):
-        lo, hi = t * TILE, (t + 1) * TILE
-        rows = [work[lo + GROUP * i : lo + GROUP * (i + 1), lo:hi] for i in range(TILE // GROUP)]
-        inverse = jnp.concatenate(inverse_tile(rows, lane, sub), axis=0)
-        solved = exact_dot(inverse, work[lo:hi, hi:])
-        for i in range(tiles):
-            if i != t:
-                span = slice(i * TILE, (i + 1) * TILE)
-                work[span, hi:] = work[span, hi:] - exact_dot(work[span, lo:hi], solved)
-        work[lo:hi, hi:] = solved
+    spans = [slice(t * TILE, (t + 1) * TILE) for t in range(tiles)]
+    held = None
+    for t in range(tiles + 1):
+        if t < tiles:
+            here, rest = spans[t], (t + 1) * TILE
+            square = work[here, here]
+            if held is not None:
+                square = square - exact_dot(work[here, spans[t - 1]], held[:, :TILE])
+            rows = [square[GROUP * i : GROUP * (i + 1)] for i in range(TILE // GROUP)]
+            inverse = jnp.concatenate(inverse_tile(rows, lane, sub), axis=0)
+        if held is not None:
+            column = slice(t * TILE, work.shape[1])
+            for i in range(tiles):
+                if i != t - 1:
+                    work[spans[i], column] = work[spans[i], column] - exact_dot(
+                        work[spans[i], spans[t - 1]], held
+                    )
+            work[spans[t - 1], column] = held
+        if t < tiles:
+            held = exact_dot(inverse, work[here, rest:])
     out_ref[...] = work[:, size:]
 
 
@@ -271,9 +281,10 @@
     block = block.reshape(-1, high, row_share, column_share)
     slab = block.transpose(1, 3, 0, 2).reshape(high * column_share, sensors)
     slabs = from_everyone(jnp.concatenate([slab, gain], axis=1), ("x", "core"))
+
+    obs = by_shifts(obs, "zl").reshape(-1, width)
     slabs, obs = lax.optimization_barrier((slabs, obs))
-
-    obs_rows = from_everyone(obs, ROW).reshape(sensors, width)
+    obs_rows = from_everyone(obs, "y").reshape(sensors, width)
     solved = solve_gain(slabs, noise_variance)
     return forecast - contract(solved, obs_rows, ((0,), (0,)))
 

time: 152 us -> 154 us (1.013)
  the two profiles are of different devices: /device:TPU:16 before, /device:TPU:1 now
where the time goes in v4:
time: 154 us
  starting transfers between devices  66.9 us (43%)
  waiting for transfers between devices  42.7 us (28%)
  Pallas kernels  24.3 us (16%)
  local copies, waits for them, and re-layouts  7.87 us (5%)
  matrix products  5.86 us (4%)
  other arithmetic  5.25 us (3%)
    ppermute x6, starting transfers between devices, from_neighbours(): return (lax.ppermute(upper, axis, up), lax.ppermute(lower, axis, down))  33.1 us
    all_to_all x3, waiting for transfers between devices, from_everyone(): return lax.all_to_all(copies, axis, split_axis=0, concat_axis=0, tiled=True)  29.2 us
    pallas_call x1, Pallas kernels, solve_gain(): pl.pallas_call(solve_kernel, out_shape=jax.ShapeDtypeStruct((size, wide -...  21.3 us
    ppermute x4, starting transfers between devices, by_shifts(): lax.ppermute(part, axis, [(i, (i + shift) % size) for i in range(size)])  18.5 us
    all_to_all x3, starting transfers between devices, from_everyone(): return lax.all_to_all(copies, axis, split_axis=0, concat_axis=0, tiled=True)  15.3 us
    ppermute x6, waiting for transfers between devices, from_neighbours(): return (lax.ppermute(upper, axis, up), lax.ppermute(lower, axis, down))  11.7 us
    dot_general x4, matrix products, contract(): return lax.dot_general(a, b, (dims, ((), ())), precision=finest_accuracy)  5.86 us
    broadcast_in_dim x3, local copies, waits for them, and re-layouts, from_everyone(): copies = jnp.broadcast_to(array, (lax.axis_size(axis), *array.shape))  3.24 us
  transfers between devices with their start and end apart: 13, of which 6 were waited for; matrix products, arithmetic and copies ran while one was open for 6% of the time, Pallas kernels for 14%

profile of v4, /device:TPU:1, one launch (start us, length us, event | category | flops | bytes accessed | tf_op | source)
XLA Modules:
  0.0 153.6 jit_solution(8676256078534681476)
XLA Ops:
  0.0 1.1 fusion.54
  1.1 11.3 %collective-permute-start.1 = (f32[256,256]{1,0:T(8,128)S(1)}, f32[256,256]{1,0:T(8,128)S(1)}, u32[]{:S(2)}, u32[]{:S(2)}) collective-permute-start(f32[256,256]{1,0:T(8,128)S(1)} %get-tuple-element.40), channel_id=1, source_target_pairs={{16,0},{32,16},{48,32},{64,48},{80,64},{96,80},{112,96},{128,112},... | collective-permute-start | bytes 786440 | tf_op jit(solution)/shard_map/ppermute | solution.py:29
  12.4 1.9 %collective-permute-start = (f32[256,256]{1,0:T(8,128)S(1)}, f32[256,256]{1,0:T(8,128)S(1)}, u32[]{:S(2)}, u32[]{:S(2)}) collective-permute-start(f32[256,256]{1,0:T(8,128)S(1)} %get-tuple-element.40), channel_id=1, source_target_pairs={{0,16},{16,32},{32,48},{48,64},{64,80},{80,96},{96,112},{112,128},... | collective-permute-start | bytes 786440 | tf_op jit(solution)/shard_map/ppermute | solution.py:29
  14.4 1.9 %collective-permute-start.3 = (f32[256,256]{1,0:T(8,128)S(1)}, f32[256,256]{1,0:T(8,128)S(1)}, u32[]{:S(2)}, u32[]{:S(2)}) collective-permute-start(f32[256,256]{1,0:T(8,128)S(1)} %get-tuple-element.39), channel_id=1, source_target_pairs={{0,16},{16,32},{32,48},{48,64},{64,80},{80,96},{96,112},{112,128},... | collective-permute-start | bytes 786440 | tf_op jit(solution)/shard_map/ppermute | solution.py:29
  16.3 7.3 %collective-permute-start.4 = (f32[256,256]{1,0:T(8,128)S(1)}, f32[256,256]{1,0:T(8,128)S(1)}, u32[]{:S(2)}, u32[]{:S(2)}) collective-permute-start(f32[256,256]{1,0:T(8,128)S(1)} %get-tuple-element.39), channel_id=1, source_target_pairs={{16,0},{32,16},{48,32},{64,48},{80,64},{96,80},{112,96},{128,112},... | collective-permute-start | bytes 786440 | tf_op jit(solution)/shard_map/ppermute | solution.py:29
  23.6 0.8 slice_bitcast_fusion.3
  24.6 0.6 fusion.34.refs_7_
  25.9 1.9 %collective-permute-done = f32[256,256]{1,0:T(8,128)S(1)} collective-permute-done((f32[256,256]{1,0:T(8,128)S(1)}, f32[256,256]{1,0:T(8,128)S(1)}, u32[]{:S(2)}, u32[]{:S(2)}) %collective-permute-start) | collective-permute-done | bytes 262176 | tf_op jit(solution)/shard_map/ppermute | solution.py:29
  29.4 8.6 %collective-permute-start.2 = (f32[256,256]{1,0:T(8,128)S(1)}, f32[256,256]{1,0:T(8,128)S(1)}, u32[]{:S(2)}, u32[]{:S(2)}) collective-permute-start(f32[256,256]{1,0:T(8,128)S(1)} %bitcast.47), channel_id=1, source_target_pairs={{0,1},{1,2},{2,3},{3,4},{4,5},{5,6},{6,7},{7,8},{8,9},{9,10},{10,1... | collective-permute-start | bytes 786440 | tf_op jit(solution)/shard_map/ppermute | solution.py:29
  39.7 2.1 %collective-permute-start.5 = (f32[256,256]{1,0:T(8,128)S(1)}, f32[256,256]{1,0:T(8,128)S(1)}, u32[]{:S(2)}, u32[]{:S(2)}) collective-permute-start(f32[256,256]{1,0:T(8,128)S(1)} %bitcast.49), channel_id=1, source_target_pairs={{1,0},{2,1},{3,2},{4,3},{5,4},{6,5},{7,6},{8,7},{9,8},{10,9},{11,1... | collective-permute-start | bytes 786440 | tf_op jit(solution)/shard_map/ppermute | solution.py:29
  42.5 0.6 fusion.30
  43.2 9.9 %collective-permute-done.5.refs_3_ = f32[256,256]{1,0:T(8,128)S(1)} collective-permute-done((f32[256,256]{1,0:T(8,128)S(1)}, f32[256,256]{1,0:T(8,128)S(1)}, u32[]{:S(2)}, u32[]{:S(2)}) %collective-permute-start.5) | collective-permute-done | bytes 262176 | tf_op jit(solution)/shard_map/ppermute | solution.py:29
  53.0 0.7 copy-done.5
  53.7 3.0 %columns_forecast.1 = f32[256,512]{1,0:T(8,128)} custom-call(f32[256,256]{1,0:T(8,128)} %copy-done.4, f32[256,256]{1,0:T(8,128)} %bitcast.50, f32[256,256]{1,0:T(8,128)} %bitcast.48, f32[256,256]{1,0:T(8,128)} %copy-done.5, f32[8,128]{1,0:T(8,128)} %fusion.32.refs_4_, f32[6,128]{1,0:T(8,128)} %get-tuple-element.61.refs_5_, ...), custom_call_target="tpu_custom_call" | custom-call | tf_op jit(solution)/shard_map/columns_forecast/pallas_call | solution.py:199
  56.8 1.4 bitcast_dynamic-update-slice_fusion.5
  58.2 9.5 %collective-permute-start.6 = (f32[32,256]{1,0:T(8,128)S(1)}, f32[32,256]{1,0:T(8,128)S(1)}, u32[]{:S(2)}, u32[]{:S(2)}) collective-permute-start(f32[32,256]{1,0:T(8,128)S(1)} %get-tuple-element.60), channel_id=1, source_target_pairs={{0,2},{2,0},{1,3},{3,1},{4,6},{6,4},{5,7},{7,5},{8,10},{10,8},{9,1... | collective-permute-start | bytes 98312 | tf_op jit(solution)/shard_map/ppermute | solution.py:225
  67.7 1.3 fusion.24
  69.4 0.7 broadcast_in_dim.56
  70.1 7.2 %all-to-all-start = ((f32[64,4,128]{2,1,0:T(4,128)}), f32[64,4,128]{2,1,0:T(4,128)S(1)}, u32[]{:S(2)}, u32[]{:S(2)}) async-start(f32[64,4,128]{2,1,0:T(4,128)} %broadcast_in_dim.56), calls=%async_computation | async-start | bytes 262144 | tf_op jit(solution)/shard_map/all_to_all | solution.py:22
  77.3 11.9 %all-to-all-done = f32[64,4,128]{2,1,0:T(4,128)S(1)} async-done(((f32[64,4,128]{2,1,0:T(4,128)}), f32[64,4,128]{2,1,0:T(4,128)S(1)}, u32[]{:S(2)}, u32[]{:S(2)}) %all-to-all-start) | async-done | bytes 131104 | tf_op jit(solution)/shard_map/all_to_all | solution.py:22
  90.2 1.3 broadcast_in_dim.60
  91.6 4.4 %all-to-all-start.1 = ((f32[8,64,768]{2,1,0:T(8,128)}), f32[8,64,768]{2,1,0:T(8,128)S(1)}, u32[]{:S(2)}, u32[]{:S(2)}) async-start(f32[8,64,768]{2,1,0:T(8,128)} %broadcast_in_dim.60), calls=%async_computation.1 | async-start | bytes 3145728 | tf_op jit(solution)/shard_map/all_to_all | solution.py:22
  95.9 2.2 %collective-permute-start.7 = (f32[16,512]{1,0:T(8,128)S(1)}, f32[16,512]{1,0:T(8,128)S(1)}, u32[]{:S(2)}, u32[]{:S(2)}) collective-permute-start(f32[16,512]{1,0:T(8,128)S(1)} %fusion.24), channel_id=1, source_target_pairs={{0,16},{16,32},{32,48},{48,0},{1,17},{17,33},{33,49},{49,1},{2,18}... | collective-permute-start | bytes 98312 | tf_op jit(solution)/shard_map/ppermute | solution.py:225
  98.1 2.3 %collective-permute-start.8 = (f32[16,512]{1,0:T(8,128)S(1)}, f32[16,512]{1,0:T(8,128)S(1)}, u32[]{:S(2)}, u32[]{:S(2)}) collective-permute-start(f32[16,512]{1,0:T(8,128)S(1)} %fusion.24), channel_id=1, source_target_pairs={{0,32},{16,48},{32,0},{48,16},{1,33},{17,49},{33,1},{49,17},{2,34}... | collective-permute-start | bytes 98312 | tf_op jit(solution)/shard_map/ppermute | solution.py:225
  100.4 4.5 %collective-permute-start.9 = (f32[16,512]{1,0:T(8,128)S(1)}, f32[16,512]{1,0:T(8,128)S(1)}, u32[]{:S(2)}, u32[]{:S(2)}) collective-permute-start(f32[16,512]{1,0:T(8,128)S(1)} %fusion.24), channel_id=1, source_target_pairs={{0,48},{16,0},{32,16},{48,32},{1,49},{17,1},{33,17},{49,33},{2,50}... | collective-permute-start | bytes 98312 | tf_op jit(solution)/shard_map/ppermute | solution.py:225
  105.0 1.8 %collective-permute-done.9 = f32[16,512]{1,0:T(8,128)S(1)} collective-permute-done((f32[16,512]{1,0:T(8,128)S(1)}, f32[16,512]{1,0:T(8,128)S(1)}, u32[]{:S(2)}, u32[]{:S(2)}) %collective-permute-start.9) | collective-permute-done | bytes 32800 | tf_op jit(solution)/shard_map/ppermute | solution.py:225
  106.8 9.7 %all-to-all-done.1.slabs_ref = f32[8,64,768]{2,1,0:T(8,128)S(1)} async-done(((f32[8,64,768]{2,1,0:T(8,128)}), f32[8,64,768]{2,1,0:T(8,128)S(1)}, u32[]{:S(2)}, u32[]{:S(2)}) %all-to-all-start.1) | async-done | bytes 1572896 | tf_op jit(solution)/shard_map/all_to_all | solution.py:22
  116.5 1.2 broadcast_in_dim.67
  118.0 3.7 %all-to-all-start.2 = ((f32[8,64,512]{2,1,0:T(8,128)}), f32[8,64,512]{2,1,0:T(8,128)S(1)}, u32[]{:S(2)}, u32[]{:S(2)}) async-start(f32[8,64,512]{2,1,0:T(8,128)} %broadcast_in_dim.67), calls=%async_computation.2 | async-start | bytes 2097152 | tf_op jit(solution)/shard_map/all_to_all | solution.py:22
  121.8 21.3 %solve_gain.1 = f32[512,256]{1,0:T(8,128)} custom-call(f32[8,64,768]{2,1,0:T(8,128)} %copy-done.1, f32[1,512]{1,0:T(1,128)} %bitcast.55), custom_call_target="tpu_custom_call" | custom-call | tf_op jit(solution)/shard_map/solve_gain/pallas_call | solution.py:152
  143.1 7.6 %all-to-all-done.2 = f32[8,64,512]{2,1,0:T(8,128)S(1)} async-done(((f32[8,64,512]{2,1,0:T(8,128)}), f32[8,64,512]{2,1,0:T(8,128)S(1)}, u32[]{:S(2)}, u32[]{:S(2)}) %all-to-all-start.2) | async-done | bytes 1048608 | tf_op jit(solution)/shard_map/all_to_all | solution.py:22
  150.7 2.9 %convolution_subtract_fusion = f32[256,512]{1,0:T(8,128)} fusion(f32[256,512]{1,0:T(8,128)S(1)} %copy-done, f32[512,256]{1,0:T(8,128)} %solve_gain.1, f32[512,512]{1,0:T(8,128)S(1)} %bitcast.45), kind=kOutput, calls=%fused_computation | convolution fusion | flops 805437440 | bytes 2621440 | tf_op jit(solution)/shard_map/dot_general | solution.py:210
  (70 shorter events, 6.3 us)
Async XLA Ops:
  0.0 25.2 %copy-start.6 = (f32[2,128]{1,0:T(2,128)S(1)}, f32[2,128]{1,0:T(2,128)}, u32[]{:S(2)}) copy-start(f32[2,128]{1,0:T(2,128)} %param.7) | copy-start | bytes 3076
  1.1 24.8 %collective-permute-start.1 = (f32[256,256]{1,0:T(8,128)S(1)}, f32[256,256]{1,0:T(8,128)S(1)}, u32[]{:S(2)}, u32[]{:S(2)}) collective-permute-start(f32[256,256]{1,0:T(8,128)S(1)} %get-tuple-element.40), channel_id=1, source_target_pairs={{16,0},{32,16},{48,32},{64,48},{80,64},{96,80},{112,96},{128,112},... | collective-permute-start | bytes 786440 | tf_op jit(solution)/shard_map/ppermute | solution.py:29
  12.4 15.3 %collective-permute-start = (f32[256,256]{1,0:T(8,128)S(1)}, f32[256,256]{1,0:T(8,128)S(1)}, u32[]{:S(2)}, u32[]{:S(2)}) collective-permute-start(f32[256,256]{1,0:T(8,128)S(1)} %get-tuple-element.40), channel_id=1, source_target_pairs={{0,16},{16,32},{32,48},{48,64},{64,80},{80,96},{96,112},{112,128},... | collective-permute-start | bytes 786440 | tf_op jit(solution)/shard_map/ppermute | solution.py:29
  14.4 23.6 %collective-permute-start.3 = (f32[256,256]{1,0:T(8,128)S(1)}, f32[256,256]{1,0:T(8,128)S(1)}, u32[]{:S(2)}, u32[]{:S(2)}) collective-permute-start(f32[256,256]{1,0:T(8,128)S(1)} %get-tuple-element.39), channel_id=1, source_target_pairs={{0,16},{16,32},{32,48},{48,64},{64,80},{80,96},{96,112},{112,128},... | collective-permute-start | bytes 786440 | tf_op jit(solution)/shard_map/ppermute | solution.py:29
  16.3 21.7 %collective-permute-start.4 = (f32[256,256]{1,0:T(8,128)S(1)}, f32[256,256]{1,0:T(8,128)S(1)}, u32[]{:S(2)}, u32[]{:S(2)}) collective-permute-start(f32[256,256]{1,0:T(8,128)S(1)} %get-tuple-element.39), channel_id=1, source_target_pairs={{16,0},{32,16},{48,32},{64,48},{80,64},{96,80},{112,96},{128,112},... | collective-permute-start | bytes 786440 | tf_op jit(solution)/shard_map/ppermute | solution.py:29
  29.4 8.8 %copy-start.2 = (f32[2,128,256]{2,1,0:T(8,128)}, f32[2,128,256]{2,1,0:T(8,128)S(1)}, u32[]{:S(2)}) copy-start(f32[2,128,256]{2,1,0:T(8,128)S(1)} %fusion.14) | copy-start | bytes 786436
  29.4 13.8 %collective-permute-start.2 = (f32[256,256]{1,0:T(8,128)S(1)}, f32[256,256]{1,0:T(8,128)S(1)}, u32[]{:S(2)}, u32[]{:S(2)}) collective-permute-start(f32[256,256]{1,0:T(8,128)S(1)} %bitcast.47), channel_id=1, source_target_pairs={{0,1},{1,2},{2,3},{3,4},{4,5},{5,6},{6,7},{7,8},{8,9},{9,10},{10,1... | collective-permute-start | bytes 786440 | tf_op jit(solution)/shard_map/ppermute | solution.py:29
  39.0 2.8 %copy-start.7 = (s32[512]{0:T(512)S(1)}, s32[512]{0:T(512)}, u32[]{:S(2)}) copy-start(s32[512]{0:T(512)} %param.8) | copy-start | bytes 6148
  39.7 13.4 %copy-start.3 = (f32[2,128,256]{2,1,0:T(8,128)}, f32[2,128,256]{2,1,0:T(8,128)S(1)}, u32[]{:S(2)}) copy-start(f32[2,128,256]{2,1,0:T(8,128)S(1)} %fusion.12) | copy-start | bytes 786436
  39.7 13.4 %collective-permute-start.5 = (f32[256,256]{1,0:T(8,128)S(1)}, f32[256,256]{1,0:T(8,128)S(1)}, u32[]{:S(2)}, u32[]{:S(2)}) collective-permute-start(f32[256,256]{1,0:T(8,128)S(1)} %bitcast.49), channel_id=1, source_target_pairs={{1,0},{2,1},{3,2},{4,3},{5,4},{6,5},{7,6},{8,7},{9,8},{10,9},{11,1... | collective-permute-start | bytes 786440 | tf_op jit(solution)/shard_map/ppermute | solution.py:29
  43.2 9.9 %copy-start.4 = (f32[256,256]{1,0:T(8,128)}, f32[256,256]{1,0:T(8,128)S(1)}, u32[]{:S(2)}) copy-start(f32[256,256]{1,0:T(8,128)S(1)} %collective-permute-done.2.refs_0_) | copy-start | bytes 786436
  53.0 0.7 copy-start.5
  58.2 19.1 %collective-permute-start.6 = (f32[32,256]{1,0:T(8,128)S(1)}, f32[32,256]{1,0:T(8,128)S(1)}, u32[]{:S(2)}, u32[]{:S(2)}) collective-permute-start(f32[32,256]{1,0:T(8,128)S(1)} %get-tuple-element.60), channel_id=1, source_target_pairs={{0,2},{2,0},{1,3},{3,1},{4,6},{6,4},{5,7},{7,5},{8,10},{10,8},{9,1... | collective-permute-start | bytes 98312 | tf_op jit(solution)/shard_map/ppermute | solution.py:225
  70.1 19.1 %all-to-all-start = ((f32[64,4,128]{2,1,0:T(4,128)}), f32[64,4,128]{2,1,0:T(4,128)S(1)}, u32[]{:S(2)}, u32[]{:S(2)}) async-start(f32[64,4,128]{2,1,0:T(4,128)} %broadcast_in_dim.56), calls=%async_computation | async-start | bytes 262144 | tf_op jit(solution)/shard_map/all_to_all | solution.py:22
  91.6 25.0 %all-to-all-start.1 = ((f32[8,64,768]{2,1,0:T(8,128)}), f32[8,64,768]{2,1,0:T(8,128)S(1)}, u32[]{:S(2)}, u32[]{:S(2)}) async-start(f32[8,64,768]{2,1,0:T(8,128)} %broadcast_in_dim.60), calls=%async_computation.1 | async-start | bytes 3145728 | tf_op jit(solution)/shard_map/all_to_all | solution.py:22
  95.9 9.1 %collective-permute-start.7 = (f32[16,512]{1,0:T(8,128)S(1)}, f32[16,512]{1,0:T(8,128)S(1)}, u32[]{:S(2)}, u32[]{:S(2)}) collective-permute-start(f32[16,512]{1,0:T(8,128)S(1)} %fusion.24), channel_id=1, source_target_pairs={{0,16},{16,32},{32,48},{48,0},{1,17},{17,33},{33,49},{49,1},{2,18}... | collective-permute-start | bytes 98312 | tf_op jit(solution)/shard_map/ppermute | solution.py:225
  98.1 6.9 %collective-permute-start.8 = (f32[16,512]{1,0:T(8,128)S(1)}, f32[16,512]{1,0:T(8,128)S(1)}, u32[]{:S(2)}, u32[]{:S(2)}) collective-permute-start(f32[16,512]{1,0:T(8,128)S(1)} %fusion.24), channel_id=1, source_target_pairs={{0,32},{16,48},{32,0},{48,16},{1,33},{17,49},{33,1},{49,17},{2,34}... | collective-permute-start | bytes 98312 | tf_op jit(solution)/shard_map/ppermute | solution.py:225
  100.4 6.4 %collective-permute-start.9 = (f32[16,512]{1,0:T(8,128)S(1)}, f32[16,512]{1,0:T(8,128)S(1)}, u32[]{:S(2)}, u32[]{:S(2)}) collective-permute-start(f32[16,512]{1,0:T(8,128)S(1)} %fusion.24), channel_id=1, source_target_pairs={{0,48},{16,0},{32,16},{48,32},{1,49},{17,1},{33,17},{49,33},{2,50}... | collective-permute-start | bytes 98312 | tf_op jit(solution)/shard_map/ppermute | solution.py:225
  116.5 1.5 copy-start.1
  118.0 32.7 %all-to-all-start.2 = ((f32[8,64,512]{2,1,0:T(8,128)}), f32[8,64,512]{2,1,0:T(8,128)S(1)}, u32[]{:S(2)}, u32[]{:S(2)}) async-start(f32[8,64,512]{2,1,0:T(8,128)} %broadcast_in_dim.67), calls=%async_computation.2 | async-start | bytes 2097152 | tf_op jit(solution)/shard_map/all_to_all | solution.py:22
  121.8 28.9 %copy-start = (f32[256,512]{1,0:T(8,128)S(1)}, f32[256,512]{1,0:T(8,128)}, u32[]{:S(2)}) copy-start(f32[256,512]{1,0:T(8,128)} %columns_forecast.1) | copy-start | bytes 1572868

commit v5 on v4

--- a/solution.py
+++ b/solution.py
@@ -106,17 +106,18 @@
     return jnp.dot(a, b, precision=finest_accuracy, preferred_element_type=jnp.float32)
 
 
-def solve_kernel(slabs_ref, noise_ref, out_ref, work):
+def solve_kernel(mine_ref, other_ref, noise_ref, core_ref, out_ref, work):
     size = noise_ref.shape[1]
     lane = lax.broadcasted_iota(jnp.int32, (GROUP, TILE), 1)
     sub = lax.broadcasted_iota(jnp.int32, (GROUP, TILE), 0)
-    slabs, share = slabs_ref.shape[0], slabs_ref.shape[1] // HALVES
-    for n in range(slabs):
-        for half in range(HALVES):
-            place = (n // CORES * HALVES + half) * CORES + n % CORES
-            work[place * share : (place + 1) * share, :] = slabs_ref[
-                n, half * share : (half + 1) * share, :
-            ]
+    share = mine_ref.shape[1] // HALVES
+    for ref, core in ((mine_ref, core_ref[0]), (other_ref, 1 - core_ref[0])):
+        for n in range(ref.shape[0]):
+            for half in range(HALVES):
+                place = (n * HALVES + half) * CORES + core
+                work[pl.ds(pl.multiple_of(place * share, share), share), :] = ref[
+                    n, half * share : (half + 1) * share, :
+                ]
     square = work[:, :size]
     square = 0.5 * (square + square.T)
     diagonal = lax.broadcasted_iota(jnp.int32, (size, size), 0) == lax.broadcasted_iota(
@@ -147,16 +148,17 @@
     out_ref[...] = work[:, size:]
 
 
-def solve_gain(slabs, noise):
-    size, wide = noise.shape[0], slabs.shape[2]
+def solve_gain(mine, other, noise, core):
+    size, wide = noise.shape[0], mine.shape[2]
     return pl.pallas_call(
         solve_kernel,
         out_shape=jax.ShapeDtypeStruct((size, wide - size), jnp.float32),
-        in_specs=[pl.BlockSpec(memory_space=pltpu.VMEM)] * 2,
+        in_specs=[pl.BlockSpec(memory_space=pltpu.VMEM)] * 3
+        + [pl.BlockSpec(memory_space=pltpu.SMEM)],
         out_specs=pl.BlockSpec(memory_space=pltpu.VMEM),
         scratch_shapes=[pltpu.VMEM((size, wide), jnp.float32)],
         name="solve_gain",
-    )(slabs, noise[None, :])
+    )(mine, other, noise[None, :], jnp.reshape(core, (1,)))
 
 
 def columns_kernel(*refs):
@@ -280,12 +282,12 @@
     block, gain, obs = lax.optimization_barrier((block, gain, obs))
     block = block.reshape(-1, high, row_share, column_share)
     slab = block.transpose(1, 3, 0, 2).reshape(high * column_share, sensors)
-    slabs = from_everyone(jnp.concatenate([slab, gain], axis=1), ("x", "core"))
-
-    obs = by_shifts(obs, "zl").reshape(-1, width)
-    slabs, obs = lax.optimization_barrier((slabs, obs))
-    obs_rows = from_everyone(obs, "y").reshape(sensors, width)
-    solved = solve_gain(slabs, noise_variance)
+    mine = from_everyone(jnp.concatenate([slab, gain], axis=1), "x")
+
+    mine, obs = lax.optimization_barrier((mine, obs))
+    other = lax.ppermute(mine, "core", [(0, 1), (1, 0)])
+    obs_rows = from_everyone(obs, ROW).reshape(sensors, width)
+    solved = solve_gain(mine, other, noise_variance, lax.axis_index("core"))
     return forecast - contract(solved, obs_rows, ((0,), (0,)))
 
 

time: 154 us -> 146 us (0.948)
  blocking collectives: 0 us -> 15.8 us
  waiting for transfers between devices: 42.7 us -> 28.5 us
  starting transfers between devices: 66.9 us -> 58.2 us
    all_to_all x0 -> x1, blocking collectives: none -> 15.8 us  [from_everyone(): return lax.all_to_all(copies, axis, split_axis=0, concat_axis=0, tiled=True)]
    all_to_all x3 -> x2, waiting for transfers between devices: 29.2 us -> 13.5 us  [from_everyone(): return lax.all_to_all(copies, axis, split_axis=0, concat_axis=0, tiled=True)]
    ppermute x4 -> x1, starting transfers between devices: 18.5 us -> 6.23 us  [by_shifts(): lax.ppermute(part, axis, [(i, (i + shift) % size) for i in range(size)])]
    ppermute x6, starting transfers between devices: 33.1 us -> 35.4 us  [from_neighbours(): return (lax.ppermute(upper, axis, up), lax.ppermute(lower, axis, down))]
    ppermute x0 -> x1, starting transfers between devices: none -> 2.26 us  [one_cycle(): other = lax.ppermute(mine, 'core', [(0, 1), (1, 0)])]
    unnamed x16 -> x20, local copies, waits for them, and re-layouts: 0.97 us -> 3.03 us
    ppermute x0 -> x1, waiting for transfers between devices: none -> 1.91 us  [one_cycle(): other = lax.ppermute(mine, 'core', [(0, 1), (1, 0)])]
    ppermute x4 -> x1, waiting for transfers between devices: 1.77 us -> 0.01 us  [by_shifts(): lax.ppermute(part, axis, [(i, (i + shift) % size) for i in range(size)])]
  transfers between devices with their start and end apart: 13 -> 10, of which waited for: 6 -> 6; matrix products, arithmetic and copies ran while one was open for 6% -> 4% of each run, Pallas kernels for 14% -> 15%
where the time goes in v5:
time: 146 us; the launch traced here: 145 us
  starting transfers between devices  58.2 us (40%)
  waiting for transfers between devices  28.5 us (20%)
  Pallas kernels  24.4 us (17%)
  blocking collectives  15.8 us (11%)
  local copies, waits for them, and re-layouts  7.79 us (5%)
  other arithmetic  5.26 us (4%)
  matrix products  4.88 us (3%)
    ppermute x6, starting transfers between devices, from_neighbours(): return (lax.ppermute(upper, axis, up), lax.ppermute(lower, axis, down))  35.4 us
    pallas_call x1, Pallas kernels, solve_gain(): pl.pallas_call(solve_kernel, out_shape=jax.ShapeDtypeStruct((size, wide -...  21.4 us
    all_to_all x1, blocking collectives, from_everyone(): return lax.all_to_all(copies, axis, split_axis=0, concat_axis=0, tiled=True)  15.8 us
    all_to_all x2, starting transfers between devices, from_everyone(): return lax.all_to_all(copies, axis, split_axis=0, concat_axis=0, tiled=True)  14.3 us
    all_to_all x2, waiting for transfers between devices, from_everyone(): return lax.all_to_all(copies, axis, split_axis=0, concat_axis=0, tiled=True)  13.5 us
    ppermute x6, waiting for transfers between devices, from_neighbours(): return (lax.ppermute(upper, axis, up), lax.ppermute(lower, axis, down))  13.1 us
    ppermute x1, starting transfers between devices, by_shifts(): lax.ppermute(part, axis, [(i, (i + shift) % size) for i in range(size)])  6.23 us
    dot_general x4, matrix products, contract(): return lax.dot_general(a, b, (dims, ((), ())), precision=finest_accuracy)  4.88 us
  transfers between devices with their start and end apart: 10, of which 6 were waited for; matrix products, arithmetic and copies ran while one was open for 4% of the time, Pallas kernels for 15%

profile of v5, /device:TPU:1, one launch (start us, length us, event | category | flops | bytes accessed | tf_op | source)
XLA Modules:
  0.0 145.5 jit_solution(2126404987144541459)
XLA Ops:
  0.0 1.1 fusion.54
  1.1 5.0 %collective-permute-start = (f32[256,256]{1,0:T(8,128)S(1)}, f32[256,256]{1,0:T(8,128)S(1)}, u32[]{:S(2)}, u32[]{:S(2)}) collective-permute-start(f32[256,256]{1,0:T(8,128)S(1)} %get-tuple-element.40), channel_id=1, source_target_pairs={{0,16},{16,32},{32,48},{48,64},{64,80},{80,96},{96,112},{112,128},... | collective-permute-start | bytes 786440 | tf_op jit(solution)/shard_map/ppermute | solution.py:29
  6.0 8.4 %collective-permute-start.1 = (f32[256,256]{1,0:T(8,128)S(1)}, f32[256,256]{1,0:T(8,128)S(1)}, u32[]{:S(2)}, u32[]{:S(2)}) collective-permute-start(f32[256,256]{1,0:T(8,128)S(1)} %get-tuple-element.40), channel_id=1, source_target_pairs={{16,0},{32,16},{48,32},{64,48},{80,64},{96,80},{112,96},{128,112},... | collective-permute-start | bytes 786440 | tf_op jit(solution)/shard_map/ppermute | solution.py:29
  14.5 1.9 %collective-permute-start.3 = (f32[256,256]{1,0:T(8,128)S(1)}, f32[256,256]{1,0:T(8,128)S(1)}, u32[]{:S(2)}, u32[]{:S(2)}) collective-permute-start(f32[256,256]{1,0:T(8,128)S(1)} %get-tuple-element.39), channel_id=1, source_target_pairs={{0,16},{16,32},{32,48},{48,64},{64,80},{80,96},{96,112},{112,128},... | collective-permute-start | bytes 786440 | tf_op jit(solution)/shard_map/ppermute | solution.py:29
  16.4 7.3 %collective-permute-start.4 = (f32[256,256]{1,0:T(8,128)S(1)}, f32[256,256]{1,0:T(8,128)S(1)}, u32[]{:S(2)}, u32[]{:S(2)}) collective-permute-start(f32[256,256]{1,0:T(8,128)S(1)} %get-tuple-element.39), channel_id=1, source_target_pairs={{16,0},{32,16},{48,32},{64,48},{80,64},{96,80},{112,96},{128,112},... | collective-permute-start | bytes 786440 | tf_op jit(solution)/shard_map/ppermute | solution.py:29
  23.9 0.6 fusion.34.refs_7_
  24.6 0.7 copy-done.8
  25.2 0.6 pad_maximum_fusion.3.refs_8_
  27.5 1.4 collective-permute-done.3
  29.0 3.3 %collective-permute-done.4 = f32[256,256]{1,0:T(8,128)S(1)} collective-permute-done((f32[256,256]{1,0:T(8,128)S(1)}, f32[256,256]{1,0:T(8,128)S(1)}, u32[]{:S(2)}, u32[]{:S(2)}) %collective-permute-start.4) | collective-permute-done | bytes 262176 | tf_op jit(solution)/shard_map/ppermute | solution.py:29
  33.2 10.9 %collective-permute-start.2 = (f32[256,256]{1,0:T(8,128)S(1)}, f32[256,256]{1,0:T(8,128)S(1)}, u32[]{:S(2)}, u32[]{:S(2)}) collective-permute-start(f32[256,256]{1,0:T(8,128)S(1)} %bitcast.39), channel_id=1, source_target_pairs={{0,1},{1,2},{2,3},{3,4},{4,5},{5,6},{6,7},{7,8},{8,9},{9,10},{10,1... | collective-permute-start | bytes 786440 | tf_op jit(solution)/shard_map/ppermute | solution.py:29
  44.8 1.9 %collective-permute-start.5 = (f32[256,256]{1,0:T(8,128)S(1)}, f32[256,256]{1,0:T(8,128)S(1)}, u32[]{:S(2)}, u32[]{:S(2)}) collective-permute-start(f32[256,256]{1,0:T(8,128)S(1)} %bitcast.41), channel_id=1, source_target_pairs={{1,0},{2,1},{3,2},{4,3},{5,4},{6,5},{7,6},{8,7},{9,8},{10,9},{11,1... | collective-permute-start | bytes 786440 | tf_op jit(solution)/shard_map/ppermute | solution.py:29
  46.8 0.7 copy-done.9
  47.6 0.6 fusion.32.refs_4_
  48.2 0.6 fusion.30
  48.8 8.4 %collective-permute-done.5.refs_3_ = f32[256,256]{1,0:T(8,128)S(1)} collective-permute-done((f32[256,256]{1,0:T(8,128)S(1)}, f32[256,256]{1,0:T(8,128)S(1)}, u32[]{:S(2)}, u32[]{:S(2)}) %collective-permute-start.5) | collective-permute-done | bytes 262176 | tf_op jit(solution)/shard_map/ppermute | solution.py:29
  57.2 0.7 copy-done.6
  58.0 3.0 %columns_forecast.1 = f32[256,512]{1,0:T(8,128)} custom-call(f32[256,256]{1,0:T(8,128)} %copy-done.5, f32[256,256]{1,0:T(8,128)} %bitcast.42, f32[256,256]{1,0:T(8,128)} %bitcast.40, f32[256,256]{1,0:T(8,128)} %copy-done.6, f32[8,128]{1,0:T(8,128)} %fusion.32.refs_4_, f32[6,128]{1,0:T(8,128)} %get-tuple-element.61.refs_5_, ...), custom_call_target="tpu_custom_call" | custom-call | tf_op jit(solution)/shard_map/columns_forecast/pallas_call | solution.py:201
  61.0 1.5 %bitcast_dynamic-update-slice_fusion.1 = (f32[2,32,256]{2,1,0:T(8,128)S(1)}, f32[32,256]{1,0:T(8,128)S(1)}) fusion(f32[2,32,256]{2,1,0:T(8,128)S(1)} %broadcast_in_dim.41, s32[]{:T(128)S(6)} %select_n.136, f32[256,512]{1,0:T(8,128)} %columns_forecast.1, s32[512]{0:T(512)S(1)} %iota_add_fusion, s32[32]{0:T(128)S(1)} %dynamic_slice.43), kind=kOutput, calls=%fused_computation.61 | convolution fusion | flops 50348032 | bytes 592388 | tf_op jit(solution)/shard_map/dot_general | solution.py:212
  62.5 6.2 %collective-permute-start.6 = (f32[32,256]{1,0:T(8,128)S(1)}, f32[32,256]{1,0:T(8,128)S(1)}, u32[]{:S(2)}, u32[]{:S(2)}) collective-permute-start(f32[32,256]{1,0:T(8,128)S(1)} %get-tuple-element.60), channel_id=1, source_target_pairs={{0,2},{2,0},{1,3},{3,1},{4,6},{6,4},{5,7},{7,5},{8,10},{10,8},{9,1... | collective-permute-start | bytes 98312 | tf_op jit(solution)/shard_map/ppermute | solution.py:227
  69.4 0.7 broadcast_in_dim.40
  70.1 10.4 %all-to-all-start = ((f32[64,4,128]{2,1,0:T(4,128)}), f32[64,4,128]{2,1,0:T(4,128)S(1)}, u32[]{:S(2)}, u32[]{:S(2)}) async-start(f32[64,4,128]{2,1,0:T(4,128)} %broadcast_in_dim.40), calls=%async_computation | async-start | bytes 262144 | tf_op jit(solution)/shard_map/all_to_all | solution.py:22
  80.5 11.9 %all-to-all-done = f32[64,4,128]{2,1,0:T(4,128)S(1)} async-done(((f32[64,4,128]{2,1,0:T(4,128)}), f32[64,4,128]{2,1,0:T(4,128)S(1)}, u32[]{:S(2)}, u32[]{:S(2)}) %all-to-all-start) | async-done | bytes 131104 | tf_op jit(solution)/shard_map/all_to_all | solution.py:22
  93.5 15.8 %all_to_all.15.mine_ref = f32[4,64,768]{2,1,0:T(8,128)S(1)} all-to-all(f32[4,64,768]{2,1,0:T(8,128)S(1)} %broadcast_in_dim.44), channel_id=1, replica_groups=mesh['y'=8,'zl'=4,'x'=4,'zh'=2,'core'=2] {'x'}, dimensions={0} | all-to-all | bytes 1572864 | tf_op jit(solution)/shard_map/all_to_all | solution.py:22
  109.4 1.2 broadcast_in_dim.46
  110.6 3.9 %all-to-all-start.2 = ((f32[32,16,512]{2,1,0:T(8,128)}), f32[32,16,512]{2,1,0:T(8,128)S(1)}, u32[]{:S(2)}, u32[]{:S(2)}) async-start(f32[32,16,512]{2,1,0:T(8,128)} %broadcast_in_dim.46), calls=%async_computation.2 | async-start | bytes 2097152 | tf_op jit(solution)/shard_map/all_to_all | solution.py:22
  114.5 2.3 %collective-permute-start.7 = (f32[4,64,768]{2,1,0:T(8,128)S(1)}, f32[4,64,768]{2,1,0:T(8,128)S(1)}, u32[]{:S(2)}, u32[]{:S(2)}) collective-permute-start(f32[4,64,768]{2,1,0:T(8,128)S(1)} %all_to_all.15.mine_ref), channel_id=1, source_target_pairs={{0,1},{1,0},{2,3},{3,2},{4,5},{5,4},{6,7},{7,6},{8,9},{9,8},{10,11... | collective-permute-start | bytes 2359304 | tf_op jit(solution)/shard_map/ppermute | solution.py:288
  116.8 1.9 %collective-permute-done.7.other_ref = f32[4,64,768]{2,1,0:T(8,128)S(1)} collective-permute-done((f32[4,64,768]{2,1,0:T(8,128)S(1)}, f32[4,64,768]{2,1,0:T(8,128)S(1)}, u32[]{:S(2)}, u32[]{:S(2)}) %collective-permute-start.7) | collective-permute-done | bytes 786464 | tf_op jit(solution)/shard_map/ppermute | solution.py:288
  118.7 0.9 copy-done.4
  119.6 21.4 %solve_gain.1 = f32[512,256]{1,0:T(8,128)} custom-call(f32[4,64,768]{2,1,0:T(8,128)} %copy-done.1, f32[4,64,768]{2,1,0:T(8,128)} %copy-done.4, f32[1,512]{1,0:T(1,128)} %bitcast.46, s32[1]{0:T(128)} %bitcast.16.core_ref), custom_call_target="tpu_custom_call" | custom-call | tf_op jit(solution)/shard_map/solve_gain/pallas_call | solution.py:153
  141.0 1.6 %all-to-all-done.2 = f32[32,16,512]{2,1,0:T(8,128)S(1)} async-done(((f32[32,16,512]{2,1,0:T(8,128)}), f32[32,16,512]{2,1,0:T(8,128)S(1)}, u32[]{:S(2)}, u32[]{:S(2)}) %all-to-all-start.2) | async-done | bytes 1048608 | tf_op jit(solution)/shard_map/all_to_all | solution.py:22
  142.6 2.9 %convolution_subtract_fusion = f32[256,512]{1,0:T(8,128)} fusion(f32[256,512]{1,0:T(8,128)S(1)} %copy-done, f32[512,256]{1,0:T(8,128)} %solve_gain.1, f32[512,512]{1,0:T(8,128)S(1)} %bitcast.37), kind=kOutput, calls=%fused_computation | convolution fusion | flops 805437440 | bytes 2621440 | tf_op jit(solution)/shard_map/dot_general | solution.py:212
  (64 shorter events, 5.3 us)
Async XLA Ops:
  1.1 22.7 %copy-start.7 = (f32[2,2,64,128]{3,2,1,0:T(8,128)S(1)}, f32[2,2,64,128]{3,2,1,0:T(8,128)}, u32[]{:S(2)}) copy-start(f32[2,2,64,128]{3,2,1,0:T(8,128)} %param.6) | copy-start | bytes 393220
  1.1 24.8 %collective-permute-start = (f32[256,256]{1,0:T(8,128)S(1)}, f32[256,256]{1,0:T(8,128)S(1)}, u32[]{:S(2)}, u32[]{:S(2)}) collective-permute-start(f32[256,256]{1,0:T(8,128)S(1)} %get-tuple-element.40), channel_id=1, source_target_pairs={{0,16},{16,32},{32,48},{48,64},{64,80},{80,96},{96,112},{112,128},... | collective-permute-start | bytes 786440 | tf_op jit(solution)/shard_map/ppermute | solution.py:29
  6.0 19.8 %collective-permute-start.1 = (f32[256,256]{1,0:T(8,128)S(1)}, f32[256,256]{1,0:T(8,128)S(1)}, u32[]{:S(2)}, u32[]{:S(2)}) collective-permute-start(f32[256,256]{1,0:T(8,128)S(1)} %get-tuple-element.40), channel_id=1, source_target_pairs={{16,0},{32,16},{48,32},{64,48},{80,64},{96,80},{112,96},{128,112},... | collective-permute-start | bytes 786440 | tf_op jit(solution)/shard_map/ppermute | solution.py:29
  14.5 14.5 %collective-permute-start.3 = (f32[256,256]{1,0:T(8,128)S(1)}, f32[256,256]{1,0:T(8,128)S(1)}, u32[]{:S(2)}, u32[]{:S(2)}) collective-permute-start(f32[256,256]{1,0:T(8,128)S(1)} %get-tuple-element.39), channel_id=1, source_target_pairs={{0,16},{16,32},{32,48},{48,64},{64,80},{80,96},{96,112},{112,128},... | collective-permute-start | bytes 786440 | tf_op jit(solution)/shard_map/ppermute | solution.py:29
  16.4 15.8 %collective-permute-start.4 = (f32[256,256]{1,0:T(8,128)S(1)}, f32[256,256]{1,0:T(8,128)S(1)}, u32[]{:S(2)}, u32[]{:S(2)}) collective-permute-start(f32[256,256]{1,0:T(8,128)S(1)} %get-tuple-element.39), channel_id=1, source_target_pairs={{16,0},{32,16},{48,32},{64,48},{80,64},{96,80},{112,96},{128,112},... | collective-permute-start | bytes 786440 | tf_op jit(solution)/shard_map/ppermute | solution.py:29
  24.6 0.7 copy-start.8
  27.5 5.7 %copy-start.2 = (f32[2,128,256]{2,1,0:T(8,128)}, f32[2,128,256]{2,1,0:T(8,128)S(1)}, u32[]{:S(2)}) copy-start(f32[2,128,256]{2,1,0:T(8,128)S(1)} %fusion.14) | copy-start | bytes 786436
  33.2 24.0 %collective-permute-start.2 = (f32[256,256]{1,0:T(8,128)S(1)}, f32[256,256]{1,0:T(8,128)S(1)}, u32[]{:S(2)}, u32[]{:S(2)}) collective-permute-start(f32[256,256]{1,0:T(8,128)S(1)} %bitcast.39), channel_id=1, source_target_pairs={{0,1},{1,2},{2,3},{3,4},{4,5},{5,6},{6,7},{7,8},{8,9},{9,10},{10,1... | collective-permute-start | bytes 786440 | tf_op jit(solution)/shard_map/ppermute | solution.py:29
  44.8 12.4 %copy-start.3 = (f32[2,128,256]{2,1,0:T(8,128)}, f32[2,128,256]{2,1,0:T(8,128)S(1)}, u32[]{:S(2)}) copy-start(f32[2,128,256]{2,1,0:T(8,128)S(1)} %fusion.12) | copy-start | bytes 786436
  44.8 12.4 %collective-permute-start.5 = (f32[256,256]{1,0:T(8,128)S(1)}, f32[256,256]{1,0:T(8,128)S(1)}, u32[]{:S(2)}, u32[]{:S(2)}) collective-permute-start(f32[256,256]{1,0:T(8,128)S(1)} %bitcast.41), channel_id=1, source_target_pairs={{1,0},{2,1},{3,2},{4,3},{5,4},{6,5},{7,6},{8,7},{9,8},{10,9},{11,1... | collective-permute-start | bytes 786440 | tf_op jit(solution)/shard_map/ppermute | solution.py:29
  46.8 0.7 copy-start.9
  57.2 0.7 copy-start.6
  57.2 0.8 copy-start.5
  61.0 7.7 %copy-start = (f32[256,512]{1,0:T(8,128)S(1)}, f32[256,512]{1,0:T(8,128)}, u32[]{:S(2)}) copy-start(f32[256,512]{1,0:T(8,128)} %columns_forecast.1) | copy-start | bytes 1572868
  62.5 18.0 %collective-permute-start.6 = (f32[32,256]{1,0:T(8,128)S(1)}, f32[32,256]{1,0:T(8,128)S(1)}, u32[]{:S(2)}, u32[]{:S(2)}) collective-permute-start(f32[32,256]{1,0:T(8,128)S(1)} %get-tuple-element.60), channel_id=1, source_target_pairs={{0,2},{2,0},{1,3},{3,1},{4,6},{6,4},{5,7},{7,5},{8,10},{10,8},{9,1... | collective-permute-start | bytes 98312 | tf_op jit(solution)/shard_map/ppermute | solution.py:227
  70.1 22.3 %all-to-all-start = ((f32[64,4,128]{2,1,0:T(4,128)}), f32[64,4,128]{2,1,0:T(4,128)S(1)}, u32[]{:S(2)}, u32[]{:S(2)}) async-start(f32[64,4,128]{2,1,0:T(4,128)} %broadcast_in_dim.40), calls=%async_computation | async-start | bytes 262144 | tf_op jit(solution)/shard_map/all_to_all | solution.py:22
  109.4 5.2 %copy-start.1 = (f32[4,64,768]{2,1,0:T(8,128)}, f32[4,64,768]{2,1,0:T(8,128)S(1)}, u32[]{:S(2)}) copy-start(f32[4,64,768]{2,1,0:T(8,128)S(1)} %all_to_all.15.mine_ref) | copy-start | bytes 2359300
  110.6 32.0 %all-to-all-start.2 = ((f32[32,16,512]{2,1,0:T(8,128)}), f32[32,16,512]{2,1,0:T(8,128)S(1)}, u32[]{:S(2)}, u32[]{:S(2)}) async-start(f32[32,16,512]{2,1,0:T(8,128)} %broadcast_in_dim.46), calls=%async_computation.2 | async-start | bytes 2097152 | tf_op jit(solution)/shard_map/all_to_all | solution.py:22
  114.5 4.2 %collective-permute-start.7 = (f32[4,64,768]{2,1,0:T(8,128)S(1)}, f32[4,64,768]{2,1,0:T(8,128)S(1)}, u32[]{:S(2)}, u32[]{:S(2)}) collective-permute-start(f32[4,64,768]{2,1,0:T(8,128)S(1)} %all_to_all.15.mine_ref), channel_id=1, source_target_pairs={{0,1},{1,0},{2,3},{3,2},{4,5},{5,4},{6,7},{7,6},{8,9},{9,8},{10,11... | collective-permute-start | bytes 2359304 | tf_op jit(solution)/shard_map/ppermute | solution.py:288
  118.7 0.9 copy-start.4
